TPU v7x, 1024 devices: a whole 8x8x8 slice. The times are simulated.
1024 devices in a mesh: loop: 32 (over y_hi, x, core), section: 32 (over y_lo, z).
Axes of the slice: x: 8, y: 8 (y_hi: 2, y_lo: 4; y = y_hi * 4 + y_lo), z: 8, core: 2. Of those that a mesh axis runs over, the one named last changes fastest.
Arguments:
- features: bfloat16 [32, 64, 128, 512], P('loop', 'section'), may hold values from -6 to 6
- weight: bfloat16 [512, 512], replicated, may hold values from -0.25 to 0.25
- edge_tiles: bfloat16 [32, 64, 9, 128, 128], P('loop', 'section')
- block_list: int32 [32, 64, 9], P('loop', 'section'), may hold values from 0 to 8, as said below
- block_count: int32 [32, 64], P('loop', 'section'), may hold values from 1 to 9, as said below
- grad_hidden: bfloat16 [32, 64, 128, 512], P('loop', 'section'), may hold values from -6 to 6
Outputs:
- hidden: bfloat16 [32, 64, 128, 512], P('loop', 'section')
- grad_features: bfloat16 [32, 64, 128, 512], P('loop', 'section')
- grad_weight: float32 [512, 512], replicated
Inputs may be any that keep to these rules, and one draw needn't show every extreme that they name: block_list[a, b] holds the block_count[a, b] slots whose tiles are nonzero, distinct and ascending, then the self slot 4 repeated; slot 4 is always listed; no slot points outside the grid. The pattern is symmetric: slot s of tile (a, b) is listed exactly when slot 8 - s of tile (a + u - 1, b + v - 1) is, and then edge_tiles of the one is the transpose of edge_tiles of the other; edge_tiles of slot 4 is symmetric. `block_count`: some tile row has all 9 tiles nonzero.
All inputs are finite; a program needn't handle non-finite values.
Results may differ from a plain program's by a relative error of at most 0.0059.
Values may be sent and summed in bfloat16 or wider, within the bound.
A program may use at most 32 MiB of HBM per device.

v0:
```python
import math

import jax
import jax.numpy as jnp
from jax import lax
from jax.sharding import PartitionSpec as P


def extended(block, sides, width):
    for axis, dim in sides:
        count = lax.axis_size(axis)
        forward = [(i, i + 1) for i in range(count - 1)]
        backward = [(target, source) for source, target in forward]
        low = lax.ppermute(
            lax.slice_in_dim(block, block.shape[dim] - width, None, axis=dim), axis, forward
        )
        high = lax.ppermute(lax.slice_in_dim(block, 0, width, axis=dim), axis, backward)
        block = jnp.concatenate([low, block, high], axis=dim)
    return block


def from_behind(block, axis, distance):
    devices = range(lax.axis_size(axis))
    route = [(i - distance, i) for i in devices if i - distance in devices]
    return lax.ppermute(block, axis, route)


def slot_mask(block_list, block_count):
    slots = jnp.arange(9, dtype=jnp.int32)
    matches = block_list[..., :, None] == slots
    listed = slots[:, None] < block_count[..., None, None]
    return jnp.any(matches & listed, axis=-2)


def aggregate(effective, padded, tile_rows, tile_cols):
    total = jnp.zeros((tile_rows, tile_cols) + padded.shape[2:], jnp.float32)
    for row_off in range(3):
        for col_off in range(3):
            window = padded[row_off : row_off + tile_rows, col_off : col_off + tile_cols]
            total = total + jnp.einsum(
                "abij,abjf->abif",
                effective[:, :, 3 * row_off + col_off],
                window,
                preferred_element_type=jnp.float32,
            )
    return total


def per_device(features, weight, edge_tiles, block_list, block_count, grad_hidden):
    tile_rows, tile_cols = (features.shape[0], features.shape[1])
    mask = slot_mask(block_list, block_count)
    effective = edge_tiles * mask[..., None, None].astype(jnp.bfloat16)
    projected = jnp.einsum(
        "abif,fg->abig", features, weight, preferred_element_type=jnp.float32
    ).astype(jnp.bfloat16)
    padded = extended(projected, (("loop", 0), ("section", 1)), 1)
    summed = aggregate(effective, padded, tile_rows, tile_cols)
    sigmoid_part = jax.nn.sigmoid(summed)
    hidden = (summed * sigmoid_part).astype(jnp.bfloat16)
    grad_pre = (
        grad_hidden.astype(jnp.float32) * sigmoid_part * (1.0 + summed * (1.0 - sigmoid_part))
    ).astype(jnp.bfloat16)
    pushed = jnp.zeros((tile_rows + 2, tile_cols + 2) + features.shape[2:], jnp.float32)
    for row_off in range(3):
        for col_off in range(3):
            term = jnp.einsum(
                "abji,abjf->abif",
                effective[:, :, 3 * row_off + col_off],
                grad_pre,
                preferred_element_type=jnp.float32,
            )
            pushed = pushed.at[row_off : row_off + tile_rows, col_off : col_off + tile_cols].add(
                term
            )
    for offset in (-1, 1):
        outgoing = pushed[:, 0] if offset == -1 else pushed[:, tile_cols + 1]
        arrived = from_behind(outgoing, "section", offset)
        target = tile_cols if offset == -1 else 1
        pushed = pushed.at[:, target].add(arrived)
    inner = pushed[:, 1 : tile_cols + 1]
    for offset in (-1, 1):
        outgoing = inner[0] if offset == -1 else inner[tile_rows + 1]
        arrived = from_behind(outgoing, "loop", offset)
        target = tile_rows if offset == -1 else 1
        inner = inner.at[target].add(arrived)
    back = inner[1 : tile_rows + 1].astype(jnp.bfloat16)
    grad_features = jnp.einsum(
        "abig,fg->abif", back, weight, preferred_element_type=jnp.float32
    ).astype(jnp.bfloat16)
    width = features.shape[3]
    node_rows = features.reshape(-1, width)
    back_rows = back.reshape(-1, width)
    local_term = jnp.einsum("rf,rg->fg", node_rows, back_rows, preferred_element_type=jnp.float32)
    total_nodes = (
        tile_rows * lax.axis_size("loop") * tile_cols * lax.axis_size("section") * features.shape[2]
    )
    grad_weight = lax.psum(local_term, ("loop", "section")) * (1.0 / math.sqrt(total_nodes))
    return (hidden, grad_features, grad_weight)


def solution(mesh):
    placed = (
        P("loop", "section", None, None),
        P(),
        P("loop", "section", None, None, None),
        P("loop", "section", None),
        P("loop", "section"),
        P("loop", "section", None, None),
    )
    return jax.shard_map(
        per_device,
        mesh=mesh,
        in_specs=placed,
        out_specs=(P("loop", "section", None, None), P("loop", "section", None, None), P()),
        check_vma=False,
    )
```

profile of v0, /device:TPU:1, one launch (start us, length us, event | category | flops | bytes accessed | tf_op | source)
XLA Modules:
  0.0 418.6 jit_solution(11688570654133945609)
XLA Ops:
  7.2 1.0 copy-done
  8.2 1.2 convolution_convert_fusion.1
  9.5 16.1 %collective-permute-start.1 = (bf16[1,2,128,512]{3,2,1,0:T(8,128)(2,1)S(1)}, bf16[1,2,128,512]{3,2,1,0:T(8,128)(2,1)S(1)}, u32[]{:S(2)}, u32[]{:S(2)}) collective-permute-start(bf16[1,2,128,512]{3,2,1,0:T(8,128)(2,1)S(1)} %bitcast.197), channel_id=1, source_target_pairs={{32,0},{64,32},{96,64},{128,96},{160,128},{192,160},{224,192},{256... | collective-permute-start | bytes 786440 | tf_op jit(solution)/shard_map/ppermute | solution.py:17
  25.5 1.9 collective-permute-start
  29.7 1.2 copy_multiply_fusion
  30.9 1.4 and_reduce_fusion
  33.3 1.3 collective-permute-start.3
  34.6 4.0 collective-permute-start.2
  39.0 7.2 %collective-permute-done.2 = bf16[3,1,128,512]{3,2,1,0:T(8,128)(2,1)S(1)} collective-permute-done((bf16[3,1,128,512]{3,2,1,0:T(8,128)(2,1)S(1)}, bf16[3,1,128,512]{3,2,1,0:T(8,128)(2,1)S(1)}, u32[]{:S(2)}, u32[]{:S(2)}) %collective-permute-start.2) | collective-permute-done | bytes 393248 | tf_op jit(solution)/shard_map/ppermute | solution.py:14
  48.9 1.6 fusion.7
  50.5 2.2 fusion.10
  54.5 1.3 collective-permute-start.4
  55.8 19.0 %collective-permute-done.4 = f32[3,128,512]{2,1,0:T(8,128)S(1)} collective-permute-done((f32[3,128,512]{2,1,0:T(8,128)S(1)}, f32[3,128,512]{2,1,0:T(8,128)S(1)}, u32[]{:S(2)}, u32[]{:S(2)}) %collective-permute-start.4) | collective-permute-done | bytes 786464 | tf_op jit(solution)/shard_map/ppermute | solution.py:25
  75.0 3.3 collective-permute-start.5
  78.3 14.2 %collective-permute-done.5 = f32[3,128,512]{2,1,0:T(8,128)S(1)} collective-permute-done((f32[3,128,512]{2,1,0:T(8,128)S(1)}, f32[3,128,512]{2,1,0:T(8,128)S(1)}, u32[]{:S(2)}, u32[]{:S(2)}) %collective-permute-start.5) | collective-permute-done | bytes 786464 | tf_op jit(solution)/shard_map/ppermute | solution.py:25
  92.8 1.9 collective-permute-start.7
  94.7 4.8 %collective-permute-start.6 = (f32[2,128,512]{2,1,0:T(8,128)S(1)}, f32[2,128,512]{2,1,0:T(8,128)S(1)}, u32[]{:S(2)}, u32[]{:S(2)}) collective-permute-start(f32[2,128,512]{2,1,0:T(8,128)S(1)} %get-tuple-element.165), channel_id=1, source_target_pairs={{32,0},{64,32},{96,64},{128,96},{160,128},{192,160},{224,192},{256... | collective-permute-start | bytes 1572872 | tf_op jit(solution)/shard_map/ppermute | solution.py:25
  99.5 1.3 collective-permute-done.7
  100.8 4.4 %collective-permute-done.6 = f32[2,128,512]{2,1,0:T(8,128)S(1)} collective-permute-done((f32[2,128,512]{2,1,0:T(8,128)S(1)}, f32[2,128,512]{2,1,0:T(8,128)S(1)}, u32[]{:S(2)}, u32[]{:S(2)}) %collective-permute-start.6) | collective-permute-done | bytes 524320 | tf_op jit(solution)/shard_map/ppermute | solution.py:25
  105.4 1.3 convolution_bitcast_fusion
  107.5 1.0 fusion.23
  108.6 300.6 %all-reduce.3.cloned.1.call-done = f32[512,512]{0,1:T(8,128)} async-done(((f32[512,512]{0,1:T(8,128)}), f32[512,512]{0,1:T(8,128)}) %all-reduce.3.cloned.1.call-update) | async-done | bytes 1048592 | tf_op jit(solution)/shard_map/psum | solution.py:97
  409.2 1.3 broadcast_multiply_fusion
  410.5 1.3 copy.37
  (44 shorter events, 9.6 us)
Async XLA Ops:
  7.2 1.0 copy-start
  7.2 402.0 %all-reduce.3.cloned.1.call-start = ((), (), s32[]{:S(2)}) async-start(), calls=%async_computation | async-start | bytes 2097152 | tf_op jit(solution)/shard_map/psum | solution.py:97
  9.5 23.6 %collective-permute-start.1 = (bf16[1,2,128,512]{3,2,1,0:T(8,128)(2,1)S(1)}, bf16[1,2,128,512]{3,2,1,0:T(8,128)(2,1)S(1)}, u32[]{:S(2)}, u32[]{:S(2)}) collective-permute-start(bf16[1,2,128,512]{3,2,1,0:T(8,128)(2,1)S(1)} %bitcast.197), channel_id=1, source_target_pairs={{32,0},{64,32},{96,64},{128,96},{160,128},{192,160},{224,192},{256... | collective-permute-start | bytes 786440 | tf_op jit(solution)/shard_map/ppermute | solution.py:17
  25.5 7.6 %collective-permute-start = (bf16[1,2,128,512]{3,2,1,0:T(8,128)(2,1)S(1)}, bf16[1,2,128,512]{3,2,1,0:T(8,128)(2,1)S(1)}, u32[]{:S(2)}, u32[]{:S(2)}) collective-permute-start(bf16[1,2,128,512]{3,2,1,0:T(8,128)(2,1)S(1)} %bitcast.198), channel_id=1, source_target_pairs={{0,32},{32,64},{64,96},{96,128},{128,160},{160,192},{192,224},{224... | collective-permute-start | bytes 786440 | tf_op jit(solution)/shard_map/ppermute | solution.py:14
  33.3 13.4 %collective-permute-start.3 = (bf16[3,1,128,512]{3,2,1,0:T(8,128)(2,1)S(1)}, bf16[3,1,128,512]{3,2,1,0:T(8,128)(2,1)S(1)}, u32[]{:S(2)}, u32[]{:S(2)}) collective-permute-start(bf16[3,1,128,512]{3,2,1,0:T(8,128)(2,1)S(1)} %get-tuple-element.168), channel_id=1, source_target_pairs={{1,0},{2,1},{3,2},{4,3},{5,4},{6,5},{7,6},{8,7},{9,8},{10,9},{11,1... | collective-permute-start | bytes 1179656 | tf_op jit(solution)/shard_map/ppermute | solution.py:17
  34.6 11.6 %collective-permute-start.2 = (bf16[3,1,128,512]{3,2,1,0:T(8,128)(2,1)S(1)}, bf16[3,1,128,512]{3,2,1,0:T(8,128)(2,1)S(1)}, u32[]{:S(2)}, u32[]{:S(2)}) collective-permute-start(bf16[3,1,128,512]{3,2,1,0:T(8,128)(2,1)S(1)} %get-tuple-element.167), channel_id=1, source_target_pairs={{0,1},{1,2},{2,3},{3,4},{4,5},{5,6},{6,7},{7,8},{8,9},{9,10},{10,1... | collective-permute-start | bytes 1179656 | tf_op jit(solution)/shard_map/ppermute | solution.py:14
  46.9 1.0 copy-start.2
  54.5 20.3 %collective-permute-start.4 = (f32[3,128,512]{2,1,0:T(8,128)S(1)}, f32[3,128,512]{2,1,0:T(8,128)S(1)}, u32[]{:S(2)}, u32[]{:S(2)}) collective-permute-start(f32[3,128,512]{2,1,0:T(8,128)S(1)} %slice_bitcast_fusion.1), channel_id=1, source_target_pairs={{1,0},{2,1},{3,2},{4,3},{5,4},{6,5},{7,6},{8,7},{9,8},{10,9},{11,1... | collective-permute-start | bytes 2359304 | tf_op jit(solution)/shard_map/ppermute | solution.py:25
  75.0 30.4 %copy-start.1 = (bf16[1,2,128,512]{3,2,1,0:T(8,128)(2,1)S(1)}, bf16[1,2,128,512]{3,2,1,0:T(8,128)(2,1)}, u32[]{:S(2)}) copy-start(bf16[1,2,128,512]{3,2,1,0:T(8,128)(2,1)} %param.32) | copy-start | bytes 786436
  75.0 17.4 %collective-permute-start.5 = (f32[3,128,512]{2,1,0:T(8,128)S(1)}, f32[3,128,512]{2,1,0:T(8,128)S(1)}, u32[]{:S(2)}, u32[]{:S(2)}) collective-permute-start(f32[3,128,512]{2,1,0:T(8,128)S(1)} %slice_bitcast_fusion), channel_id=1, source_target_pairs={{0,1},{1,2},{2,3},{3,4},{4,5},{5,6},{6,7},{7,8},{8,9},{9,10},{10,1... | collective-permute-start | bytes 2359304 | tf_op jit(solution)/shard_map/ppermute | solution.py:25
  92.8 8.0 %collective-permute-start.7 = (f32[2,128,512]{2,1,0:T(8,128)S(1)}, f32[2,128,512]{2,1,0:T(8,128)S(1)}, u32[]{:S(2)}, u32[]{:S(2)}) collective-permute-start(f32[2,128,512]{2,1,0:T(8,128)S(1)} %get-tuple-element.166), channel_id=1, source_target_pairs={{0,32},{32,64},{64,96},{96,128},{128,160},{160,192},{192,224},{224... | collective-permute-start | bytes 1572872 | tf_op jit(solution)/shard_map/ppermute | solution.py:25
  94.7 10.5 %collective-permute-start.6 = (f32[2,128,512]{2,1,0:T(8,128)S(1)}, f32[2,128,512]{2,1,0:T(8,128)S(1)}, u32[]{:S(2)}, u32[]{:S(2)}) collective-permute-start(f32[2,128,512]{2,1,0:T(8,128)S(1)} %get-tuple-element.165), channel_id=1, source_target_pairs={{32,0},{64,32},{96,64},{128,96},{160,128},{192,160},{224,192},{256... | collective-permute-start | bytes 1572872 | tf_op jit(solution)/shard_map/ppermute | solution.py:25
Sparse Core Ops, SparseCore 0:
  106.8 302.2 all-reduce.2
where the time goes:
time: 419 us
  waiting for transfers between devices  347 us (83%)
  starting transfers between devices  34.6 us (8%)
  between operations  14.4 us (3%)
  matrix products  11.4 us (3%)
  other arithmetic  6.97 us (2%)
  local copies, waits for them, and re-layouts  4.65 us (1%)
    psum x1, waiting for transfers between devices, per_device(): lax.psum(local_term, ('loop', 'section')) * (1.0 / math.sqrt(total_nodes))  301 us
    ppermute x4, waiting for transfers between devices, from_behind(): return lax.ppermute(block, axis, route)  38.8 us
    ppermute x2, starting transfers between devices, extended(): lax.ppermute(lax.slice_in_dim(block, 0, width, axis=dim), axis, backward)  17.4 us
    ppermute x4, starting transfers between devices, from_behind(): return lax.ppermute(block, axis, route)  11.3 us
  transfers between devices with their start and end apart: 9, of which 6 were waited for; matrix products, arithmetic and copies ran while one was open for 2% of the time, Pallas kernels for 0%

commit v1 on v0

v1 whole, which is shorter than its diff:
```python
import functools
import math

import jax
import jax.numpy as jnp
from jax import lax
from jax.experimental import pallas as pl
from jax.experimental.pallas import tpu as pltpu
from jax.sharding import PartitionSpec as P

MESH = pl.DeviceIdType.MESH
F32 = jnp.float32
BF16 = jnp.bfloat16
TILE = 128
NX, NY, NZ, NYLO = 8, 8, 8, 4
LOOP, SECTION = 2 * NX * (NY // NYLO), NYLO * NZ
DIRS = [(du, dv) for du in (-1, 0, 1) for dv in (-1, 0, 1) if (du, dv) != (0, 0)]


def dot(a, b):
    return jnp.dot(a, b, preferred_element_type=F32)


def dot_rows(a, b):
    return lax.dot_general(a, b, (((0,), (0,)), ((), ())), preferred_element_type=F32)


def dot_cols(a, b):
    return lax.dot_general(a, b, (((1,), (1,)), ((), ())), preferred_element_type=F32)


def kernel(
    blist,
    bcount,
    feat,
    weight,
    edge,
    gh,
    hid_o,
    gf_o,
    gw_o,
    w_v,
    e_v,
    gh_v,
    a_mid,
    a_side,
    acc,
    hid_v,
    gf_v,
    pc,
    ps,
    qc,
    qs,
    ax,
    axp,
    back,
    part,
    s1,
    r1,
    s2,
    r2,
    r3,
    t2,
    t1,
    tp,
    in_sem,
    out_sem,
    halo_ss,
    halo_rs,
    ghalo_ss,
    ghalo_rs,
    ax_sem,
    ar_ss,
    ar_rs,
    tp_ss,
    tp_rs,
):
    L = lax.axis_index("loop")
    S = lax.axis_index("section")
    core = lax.rem(L, 2)
    x = lax.rem(L // 2, NX)
    y = (L // (2 * NX)) * NYLO + S // NZ
    z = lax.rem(S, NZ)

    def place(px, py, pz):
        return ((py // NYLO) * (2 * NX) + px * 2 + core, lax.rem(py, NYLO) * NZ + pz)

    def peer(axis, d):
        if axis == "x":
            k = lax.rem(x + d, NX)
            return k, place(k, y, z)
        if axis == "y":
            k = lax.rem(y + d, NY)
            return k, place(x, k, z)
        k = lax.rem(z + d, NZ)
        return k, place(x, y, k)

    def inside(du, dv):
        ok = jnp.bool_(True)
        if du:
            ok = (L + du >= 0) & (L + du < LOOP)
        if dv:
            ok_v = (S + dv >= 0) & (S + dv < SECTION)
            ok = ok & ok_v if du else ok_v
        return ok

    barrier = pltpu.get_barrier_semaphore()
    for du, dv in DIRS:

        @pl.when(inside(du, dv))
        def _(du=du, dv=dv):
            pl.semaphore_signal(barrier, inc=1, device_id=(L + du, S + dv), device_id_type=MESH)

    for axis in "xyz":
        for d in range(1, 8):
            _, dev = peer(axis, d)
            pl.semaphore_signal(barrier, inc=1, device_id=dev, device_id_type=MESH)

    loads = [
        pltpu.make_async_copy(feat, pc.at[1], in_sem.at[0]),
        pltpu.make_async_copy(edge, e_v, in_sem.at[1]),
        pltpu.make_async_copy(weight, w_v, in_sem.at[2]),
        pltpu.make_async_copy(gh, gh_v, in_sem.at[3]),
    ]
    for load in loads:
        load.start()

    for mid, side in ((pc, ps), (qc, qs)):
        for du, u in ((-1, 0), (1, 2)):

            @pl.when(jnp.logical_not(inside(du, 0)))
            def _(mid=mid, side=side, u=u):
                mid[u] = jnp.zeros((2 * TILE, 512), BF16)
                for k in range(2):
                    side[k, pl.ds(u * TILE, TILE), :] = jnp.zeros((TILE, 512), BF16)

        for dv, k in ((-1, 0), (1, 1)):

            @pl.when(jnp.logical_not(inside(0, dv)))
            def _(side=side, k=k):
                side[k] = jnp.zeros((3 * TILE, 512), BF16)

    rows_in = (L > 0).astype(jnp.int32) + (L < LOOP - 1).astype(jnp.int32)
    cols_in = (S > 0).astype(jnp.int32) + (S < SECTION - 1).astype(jnp.int32)

    def halo_copy(mid, side, ss, rs, n):
        du, dv = DIRS[n]
        if dv == 0:
            src, dst = mid.at[1], mid.at[1 - du]
        elif dv == 1:
            src, dst = mid.at[1, pl.ds(TILE, TILE)], side.at[0, pl.ds((1 - du) * TILE, TILE)]
        else:
            src, dst = mid.at[1, pl.ds(0, TILE)], side.at[1, pl.ds((1 - du) * TILE, TILE)]
        return pltpu.make_async_remote_copy(
            src_ref=src,
            dst_ref=dst,
            send_sem=ss.at[n],
            recv_sem=rs.at[n],
            device_id=(L + du, S + dv),
            device_id_type=MESH,
        )

    def halo_start(mid, side, ss, rs, n, extra=None):
        du, dv = DIRS[n]
        ok = inside(du, dv)
        if extra is not None:
            ok = ok & extra

        @pl.when(ok)
        def _():
            halo_copy(mid, side, ss, rs, n).start()

    def halo_wait_recv(mid, side, ss, rs, n):
        du, dv = DIRS[n]

        @pl.when(inside(-du, -dv))
        def _():
            halo_copy(mid, side, ss, rs, n).wait_recv()

    def halo_wait_send(mid, side, ss, rs, n):
        du, dv = DIRS[n]

        @pl.when(inside(du, dv))
        def _():
            halo_copy(mid, side, ss, rs, n).wait_send()

    order = [DIRS.index(d) for d in ((-1, 0), (1, 0), (0, -1), (0, 1), (-1, -1), (-1, 1), (1, -1), (1, 1))]

    loads[0].wait()
    pl.semaphore_wait(barrier, 21 + rows_in + cols_in + rows_in * cols_in)
    for n in order:
        halo_start(pc, ps, halo_ss, halo_rs, n)

    loads[1].wait()
    for b in range(2):
        bits = jnp.int32(0)
        for k in range(9):
            bits = bits | jnp.where(k < bcount[0, b], jnp.int32(1) << blist[0, b, k], 0)
        for s in range(9):
            tile = jnp.where(((bits >> s) & 1) == 1, e_v[b, s], jnp.zeros((TILE, TILE), BF16))
            u, v = s // 3, s % 3
            col = b + v
            if col in (1, 2):
                a_mid[u, b * TILE : (b + 1) * TILE, (col - 1) * TILE : col * TILE] = tile
            else:
                a_side[b, :, u * TILE : (u + 1) * TILE] = tile

    def aggregate(mid, side, ss, rs):
        acc[...] = dot(a_mid[1], mid[1])
        for n in order[:2]:
            halo_wait_recv(mid, side, ss, rs, n)
        acc[...] += dot(a_mid[0], mid[0]) + dot(a_mid[2], mid[2])
        for n in order[2:]:
            halo_wait_recv(mid, side, ss, rs, n)
        for b in range(2):
            acc[b * TILE : (b + 1) * TILE] += dot(a_side[b], side[b])

    aggregate(pc, ps, halo_ss, halo_rs)
    for half in range(2):
        ax[half] = acc[:, half * 256 : (half + 1) * 256].astype(BF16)
    partner = (L + 1 - 2 * core, S)
    ax_copy = pltpu.make_async_remote_copy(
        src_ref=ax.at[1 - core],
        dst_ref=axp,
        send_sem=ax_sem.at[0],
        recv_sem=ax_sem.at[1],
        device_id=partner,
        device_id_type=MESH,
    )
    ax_copy.start()
    loads[2].wait()
    acc[...] = dot(ax[0], w_v[:256]) + dot(ax[1], w_v[256:])
    loads[3].wait()
    for r in range(0, 256, 32):
        p = acc[r : r + 32]
        sig = jax.nn.sigmoid(p)
        hid_v[r : r + 32] = (p * sig).astype(BF16)
        g = gh_v[r : r + 32].astype(F32)
        qc[1, r : r + 32] = (g * sig * (1.0 + p * (1.0 - sig))).astype(BF16)

    down, up = DIRS.index((-1, 0)), DIRS.index((1, 0))
    halo_start(qc, qs, ghalo_ss, ghalo_rs, up, core == 0)
    halo_start(qc, qs, ghalo_ss, ghalo_rs, down, core == 1)
    hid_out = pltpu.make_async_copy(hid_v, hid_o, out_sem.at[0])
    hid_out.start()

    own_part = dot_rows(ax[core], qc[1])
    part[...] = own_part.reshape(2, 8, 16, 512)
    ax_copy.wait()

    @pl.when(core == 0)
    def _():
        halo_wait_recv(qc, qs, ghalo_ss, ghalo_rs, down)

    @pl.when(core == 1)
    def _():
        halo_wait_recv(qc, qs, ghalo_ss, ghalo_rs, up)

    part[...] += dot_rows(axp[...], qc[2 * (1 - core)]).reshape(2, 8, 16, 512)
    s1[...] = part[...].astype(BF16)

    first = ("y", "x")
    second = ("x", "y")
    at = {"x": x, "y": y, "z": z}

    def ar(stage, h, d, src, dst, dev):
        k = (stage * 2 + h) * 7 + d - 1
        return pltpu.make_async_remote_copy(
            src_ref=src,
            dst_ref=dst,
            send_sem=ar_ss.at[k],
            recv_sem=ar_rs.at[k],
            device_id=dev,
            device_id_type=MESH,
        )

    sent = []
    both = [(h, d) for d in (4, 3, 5, 2, 6, 1, 7) for h in range(2)]

    def run(stage, make):
        copies = []
        for h, d in both:
            c = make(stage, h, d)
            c.start()
            copies.append(c)
        sent.extend(copies)
        return copies

    def make1(stage, h, d):
        k, dev = peer(first[h], d)
        return ar(stage, h, d, s1.at[h, k], r1.at[h, d - 1], dev)

    copies = run(0, make1)
    halo_start(qc, qs, ghalo_ss, ghalo_rs, up, core == 1)
    halo_start(qc, qs, ghalo_ss, ghalo_rs, down, core == 0)
    for n in order[2:]:
        halo_start(qc, qs, ghalo_ss, ghalo_rs, n)
    for c in copies:
        c.wait_recv()
    for h in range(2):
        total = part[h, at[first[h]]]
        for d in range(7):
            total = total + r1[h, d].astype(F32)
        for t in range(8):
            s2[h, t] = total[(t // 4) * 8 : (t // 4) * 8 + 8, (t % 4) * 128 : (t % 4) * 128 + 128]

    def make2(stage, h, d):
        k, dev = peer(second[h], d)
        return ar(stage, h, d, s2.at[h, k], r2.at[h, d - 1], dev)

    for c in run(1, make2):
        c.wait_recv()
    for h in range(2):
        total = s2[h, at[second[h]]]
        for d in range(7):
            total = total + r2[h, d]
        r3[h, z] = total

    def make3(stage, h, d):
        _, dev = peer("z", d)
        return ar(stage, h, d, r3.at[h, z], r3.at[h, z], dev)

    for c in run(2, make3):
        c.wait_recv()
    for h in range(2):
        total = r3[h, 0]
        for d in range(1, 8):
            total = total + r3[h, d]
        t2[h, at[second[h]]] = total

    def make4(stage, h, d):
        _, dev = peer(second[h], d)
        return ar(stage, h, d, t2.at[h, at[second[h]]], t2.at[h, at[second[h]]], dev)

    for c in run(3, make4):
        c.wait_recv()
    for h in range(2):
        lines = [jnp.concatenate([t2[h, 4 * r + k] for k in range(4)], axis=1) for r in range(2)]
        t1[h, at[first[h]]] = jnp.concatenate(lines, axis=0).astype(BF16)

    def make5(stage, h, d):
        _, dev = peer(first[h], d)
        return ar(stage, h, d, t1.at[h, at[first[h]]], t1.at[h, at[first[h]]], dev)

    copies = run(4, make5)

    aggregate_waited = [n for n in order]
    acc[...] = dot(a_mid[1], qc[1])
    for n in aggregate_waited:
        if n == down:

            @pl.when(core == 1)
            def _():
                halo_wait_recv(qc, qs, ghalo_ss, ghalo_rs, down)

        elif n == up:

            @pl.when(core == 0)
            def _():
                halo_wait_recv(qc, qs, ghalo_ss, ghalo_rs, up)

        else:
            halo_wait_recv(qc, qs, ghalo_ss, ghalo_rs, n)
    acc[...] += dot(a_mid[0], qc[0]) + dot(a_mid[2], qc[2])
    for b in range(2):
        acc[b * TILE : (b + 1) * TILE] += dot(a_side[b], qs[b])
    back[...] = acc[...].astype(BF16)
    gf_v[...] = dot_cols(back[...], w_v[...]).astype(BF16)
    gf_out = pltpu.make_async_copy(gf_v, gf_o, out_sem.at[1])
    gf_out.start()

    for c in copies:
        c.wait_recv()
    pair = pltpu.make_async_remote_copy(
        src_ref=t1,
        dst_ref=tp,
        send_sem=tp_ss,
        recv_sem=tp_rs,
        device_id=partner,
        device_id_type=MESH,
    )
    pair.start()
    own_out = pltpu.make_async_copy(t1, gw_o.at[core], out_sem.at[2])
    own_out.start()
    pair.wait_recv()
    other_out = pltpu.make_async_copy(tp, gw_o.at[1 - core], out_sem.at[3])
    other_out.start()

    for c in sent:
        c.wait_send()
    pair.wait_send()
    for n in order:
        halo_wait_send(pc, ps, halo_ss, halo_rs, n)
        halo_wait_send(qc, qs, ghalo_ss, ghalo_rs, n)
    hid_out.wait()
    gf_out.wait()
    own_out.wait()
    other_out.wait()


def per_device(features, weight, edge_tiles, block_list, block_count, grad_hidden):
    rows, width = 2 * TILE, features.shape[3]
    nodes = LOOP * SECTION * rows
    anywhere = pl.BlockSpec(memory_space=pl.ANY)
    scalars = pl.BlockSpec(memory_space=pltpu.SMEM)
    dma = pltpu.SemaphoreType.DMA
    vmem = pltpu.VMEM
    hidden, grad_features, total = pl.pallas_call(
        kernel,
        out_shape=[
            jax.ShapeDtypeStruct((rows, width), BF16),
            jax.ShapeDtypeStruct((rows, width), BF16),
            jax.ShapeDtypeStruct((2, 2, 8, 16, width), BF16),
        ],
        in_specs=[scalars, scalars, anywhere, anywhere, anywhere, anywhere],
        out_specs=[anywhere] * 3,
        scratch_shapes=[
            vmem((width, width), BF16),
            vmem((2, 9, TILE, TILE), BF16),
            vmem((rows, width), BF16),
            vmem((3, rows, rows), BF16),
            vmem((2, TILE, 3 * TILE), BF16),
            vmem((rows, width), F32),
            vmem((rows, width), BF16),
            vmem((rows, width), BF16),
            vmem((3, rows, width), BF16),
            vmem((2, 3 * TILE, width), BF16),
            vmem((3, rows, width), BF16),
            vmem((2, 3 * TILE, width), BF16),
            vmem((2, rows, 256), BF16),
            vmem((rows, 256), BF16),
            vmem((rows, width), BF16),
            vmem((2, 8, 16, width), F32),
            vmem((2, 8, 16, width), BF16),
            vmem((2, 7, 16, width), BF16),
            vmem((2, 8, 8, 128), F32),
            vmem((2, 7, 8, 128), F32),
            vmem((2, 8, 8, 128), F32),
            vmem((2, 8, 8, 128), F32),
            vmem((2, 8, 16, width), BF16),
            vmem((2, 8, 16, width), BF16),
            dma((4,)),
            dma((4,)),
            dma((8,)),
            dma((8,)),
            dma((8,)),
            dma((8,)),
            dma((2,)),
            dma((70,)),
            dma((70,)),
            dma,
            dma,
        ],
        compiler_params=pltpu.CompilerParams(collective_id=0, has_side_effects=True),
    )(
        block_list,
        block_count,
        features.reshape(rows, width),
        weight,
        edge_tiles.reshape(2, 9, TILE, TILE),
        grad_hidden.reshape(rows, width),
    )
    grad_weight = total.reshape(width, width).astype(F32) * (1.0 / math.sqrt(nodes))
    return (hidden.reshape(features.shape), grad_features.reshape(features.shape), grad_weight)


def solution(mesh):
    placed = (
        P("loop", "section", None, None),
        P(),
        P("loop", "section", None, None, None),
        P("loop", "section", None),
        P("loop", "section"),
        P("loop", "section", None, None),
    )
    return jax.shard_map(
        per_device,
        mesh=mesh,
        in_specs=placed,
        out_specs=(P("loop", "section", None, None), P("loop", "section", None, None), P()),
        check_vma=False,
    )
```

time: 419 us -> 86.1 us (0.21)
  waiting for transfers between devices: 347 us -> 0 us
  Pallas kernels: 0 us -> 81.3 us
  starting transfers between devices: 34.6 us -> 0 us
  between operations: 14.4 us -> 0.65 us
  matrix products: 11.4 us -> 0 us
  other arithmetic: 6.97 us -> 2.2 us
    psum x1 -> x0, waiting for transfers between devices: 301 us -> none  [per_device(): lax.psum(local_term, ('loop', 'section')) * (1.0 / math.sqrt(total_nodes))]
    pallas_call x0 -> x1, Pallas kernels: none -> 81.3 us  [per_device(): pl.pallas_call(kernel, out_shape=[jax.ShapeDtypeStruct((rows, width), BF1...]
    ppermute x8 -> x0, waiting for transfers between devices: 46 us -> none  [the longest x4 38.8 us: from_behind(): return lax.ppermute(block, axis, route)]
    ppermute x8 -> x0, starting transfers between devices: 34.6 us -> none  [the longest x2 17.4 us: extended(): lax.ppermute(lax.slice_in_dim(block, 0, width, axis=dim), axis, backward)]
    dot_general x21 -> x0, matrix products: 11.4 us -> none  [the longest x9 5.69 us: per_device(): jnp.einsum('abji,abjf->abif', effective[:, :, 3 * row_off + col_off], gra...]
  transfers between devices with their start and end apart: 9 -> 0, of which waited for: 6 -> 0; matrix products, arithmetic and copies ran while one was open for 2% -> 0% of each run, Pallas kernels for 0% -> 0%
where the time goes in v1:
time: 86.1 us; the launch traced here: 85.9 us
  Pallas kernels  81.3 us (94%)
  other arithmetic  2.2 us (3%)
  local copies, waits for them, and re-layouts  1.75 us (2%)
    pallas_call x1, Pallas kernels, per_device(): pl.pallas_call(kernel, out_shape=[jax.ShapeDtypeStruct((rows, width), BF1...  81.3 us
    mul x1, other arithmetic, per_device(): total.reshape(width, width).astype(F32) * (1.0 / math.sqrt(nodes))  2.2 us
    unnamed x6, local copies, waits for them, and re-layouts  1.75 us

profile of v1, /device:TPU:1, one launch (start us, length us, event | category | flops | bytes accessed | tf_op | source)
XLA Modules:
  0.0 85.9 jit_solution(15059796511535338666)
XLA Ops:
  0.6 81.3 %shard_map.85 = (bf16[256,512]{1,0:T(8,128)(2,1)}, bf16[256,512]{1,0:T(8,128)(2,1)}, bf16[2,2,8,16,512]{4,3,2,1,0:T(8,128)(2,1)}) custom-call(s32[1,2,9]{2,1,0:T(2,128)} %blist.1, s32[1,2]{1,0:T(1,128)} %bcount.1, bf16[256,512]{1,0:T(8,128)(2,1)} %bitcast.10, bf16[512,512]{1,0:T(8,128)(2,1)} %weight.1, bf16[2,9,128,128]{3,2,1,0:T(8,128)(2,1)} %bitcast.7, ...), custom_call_target="tpu_custom_call" | custom-call | tf_op jit(solution)/shard_map/pallas_call | solution.py:408
  81.9 0.0 copy-start.1
  81.9 2.2 %convert_multiply_fusion = f32[2,2,8,16,512]{4,3,2,1,0:T(8,128)} fusion(bf16[2,2,8,16,512]{4,3,2,1,0:T(8,128)(2,1)} %get-tuple-element.8), kind=kLoop, calls=%fused_computation | loop fusion | flops 524288 | bytes 1572864 | tf_op jit(solution)/shard_map/mul | solution.py:463
  84.1 0.0 copy-done.1
  84.1 0.0 copy-start
  84.1 0.7 copy.11
  84.8 0.3 copy-done
  85.2 0.7 copy.12
Async XLA Ops:
  81.9 2.2 %copy-start.1 = (bf16[256,512]{1,0:T(8,128)(2,1)S(1)}, bf16[256,512]{1,0:T(8,128)(2,1)}, u32[]{:S(2)}) copy-start(bf16[256,512]{1,0:T(8,128)(2,1)} %get-tuple-element.6) | copy-start | bytes 786436
  84.1 1.0 %copy-start = (bf16[256,512]{1,0:T(8,128)(2,1)S(1)}, bf16[256,512]{1,0:T(8,128)(2,1)}, u32[]{:S(2)}) copy-start(bf16[256,512]{1,0:T(8,128)(2,1)} %get-tuple-element.7) | copy-start | bytes 786436

commit v2 on v1

v2 whole, which is shorter than its diff:
```python
import functools
import math

import jax
import jax.numpy as jnp
from jax import lax
from jax.experimental import pallas as pl
from jax.experimental.pallas import tpu as pltpu
from jax.sharding import PartitionSpec as P

MESH = pl.DeviceIdType.MESH
F32 = jnp.float32
BF16 = jnp.bfloat16
TILE = 128
NX, NY, NZ, NYLO = 8, 8, 8, 4
LOOP, SECTION = 2 * NX * (NY // NYLO), NYLO * NZ


def dot(a, b):
    return jnp.dot(a, b, preferred_element_type=F32)


def dot_rows(a, b):
    return lax.dot_general(a, b, (((0,), (0,)), ((), ())), preferred_element_type=F32)


def dot_cols(a, b):
    return lax.dot_general(a, b, (((1,), (1,)), ((), ())), preferred_element_type=F32)


def kernel(
    scale,
    blist,
    bcount,
    feat,
    weight,
    edge,
    gh,
    hid_v,
    gf_v,
    gw_v,
    w_v,
    e_v,
    gh_v,
    a_mid,
    a_side,
    acc,
    pc,
    ps,
    qc,
    qs,
    ax,
    axp,
    back,
    part,
    s1,
    r1,
    s2,
    r2,
    r3,
    t2,
    t1,
    tp,
    in_sem,
    halo_ss,
    halo_rs,
    ghalo_ss,
    ghalo_rs,
    ax_sem,
    ar_ss,
    ar_rs,
    tp_ss,
    tp_rs,
):
    L = lax.axis_index("loop")
    S = lax.axis_index("section")
    core = lax.rem(L, 2)
    x = lax.rem(L // 2, NX)
    y = (L // (2 * NX)) * NYLO + S // NZ
    z = lax.rem(S, NZ)

    def place(px, py, pz):
        return ((py // NYLO) * (2 * NX) + px * 2 + core, lax.rem(py, NYLO) * NZ + pz)

    def peer(axis, d):
        if axis == "x":
            k = lax.rem(x + d, NX)
            return k, place(k, y, z)
        if axis == "y":
            k = lax.rem(y + d, NY)
            return k, place(x, k, z)
        k = lax.rem(z + d, NZ)
        return k, place(x, y, k)

    out_row = L - 1 + 2 * core
    partner = (L + 1 - 2 * core, S)
    has_out = (out_row >= 0) & (out_row < LOOP)
    has_side = {-1: S > 0, 1: S < SECTION - 1}
    u_out, u_in = 2 * core, 2 * (1 - core)

    barrier = pltpu.get_barrier_semaphore()
    pl.semaphore_signal(barrier, inc=1, device_id=partner, device_id_type=MESH)

    @pl.when(has_out)
    def _():
        pl.semaphore_signal(barrier, inc=1, device_id=(out_row, S), device_id_type=MESH)

    for dv in (-1, 1):

        @pl.when(has_side[dv])
        def _(dv=dv):
            pl.semaphore_signal(barrier, inc=1, device_id=(L, S + dv), device_id_type=MESH)

    for axis in "xyz":
        for d in range(1, 8):
            _, dev = peer(axis, d)
            pl.semaphore_signal(barrier, inc=1, device_id=dev, device_id_type=MESH)

    loads = [
        pltpu.make_async_copy(feat, pc.at[1], in_sem.at[0]),
        pltpu.make_async_copy(edge, e_v, in_sem.at[1]),
        pltpu.make_async_copy(weight, w_v, in_sem.at[2]),
        pltpu.make_async_copy(gh, gh_v, in_sem.at[3]),
    ]
    for load in loads:
        load.start()

    for mid, side in ((pc, ps), (qc, qs)):

        @pl.when(jnp.logical_not(has_out))
        def _(mid=mid, side=side):
            mid[u_out] = jnp.zeros((2 * TILE, 512), BF16)
            for k in range(2):
                side[k, u_out] = jnp.zeros((TILE, 512), BF16)

        for dv, k in ((-1, 0), (1, 1)):

            @pl.when(jnp.logical_not(has_side[dv]))
            def _(side=side, k=k):
                side[k] = jnp.zeros((3, TILE, 512), BF16)

    def halo(mid, side, ss, rs):
        def copy(n, src, dst, dev):
            return pltpu.make_async_remote_copy(
                src_ref=src,
                dst_ref=dst,
                send_sem=ss.at[n],
                recv_sem=rs.at[n],
                device_id=dev,
                device_id_type=MESH,
            )

        cut = {-1: pl.ds(0, TILE), 1: pl.ds(TILE, TILE)}
        slot = {-1: 1, 1: 0}
        jobs = {
            "partner": (copy(0, mid.at[1], mid.at[u_out], partner), None, None),
            "outer": (copy(1, mid.at[1], mid.at[u_in], (out_row, S)), has_out, has_out),
        }
        for i, dv in enumerate((-1, 1)):
            dev = (L, S + dv)
            jobs["side", dv] = (
                copy(2 + i, mid.at[1, cut[dv]], side.at[slot[dv], 1], dev),
                has_side[dv],
                has_side[-dv],
            )
            jobs["relay", dv] = (
                copy(4 + i, mid.at[u_out, cut[dv]], side.at[slot[dv], u_out], dev),
                has_side[dv] & has_out,
                has_side[-dv] & has_out,
            )
            jobs["share", dv] = (
                copy(6 + i, side.at[slot[dv], 1], side.at[slot[dv], u_out], partner),
                has_side[-dv],
                has_side[-dv],
            )

        def start(*keys):
            for key in keys:
                job, sends, _ = jobs[key]
                job.start() if sends is None else pl.when(sends)(job.start)

        def arrived(*keys):
            for key in keys:
                job, _, gets = jobs[key]
                job.wait_recv() if gets is None else pl.when(gets)(job.wait_recv)

        def drained():
            for job, sends, _ in jobs.values():
                job.wait_send() if sends is None else pl.when(sends)(job.wait_send)

        return start, arrived, drained

    p_start, p_arrived, p_drained = halo(pc, ps, halo_ss, halo_rs)
    q_start, q_arrived, q_drained = halo(qc, qs, ghalo_ss, ghalo_rs)
    sides = (("side", -1), ("side", 1))
    relays = (("relay", -1), ("relay", 1))
    shares = (("share", -1), ("share", 1))

    loads[0].wait()
    greeted = has_out.astype(jnp.int32) + sum(has_side[dv].astype(jnp.int32) for dv in (-1, 1))
    pl.semaphore_wait(barrier, 22 + greeted)
    p_start("outer", *sides, "partner")

    loads[1].wait()
    for b in range(2):
        bits = jnp.int32(0)
        for k in range(9):
            bits = bits | jnp.where(k < bcount[0, b], jnp.int32(1) << blist[0, b, k], 0)
        for s in range(9):
            tile = jnp.where(((bits >> s) & 1) == 1, e_v[b, s], jnp.zeros((TILE, TILE), BF16))
            u, v = s // 3, s % 3
            col = b + v
            if col in (1, 2):
                a_mid[u, b * TILE : (b + 1) * TILE, (col - 1) * TILE : col * TILE] = tile
            else:
                a_side[b, u] = tile

    def add_sides(side):
        for b in range(2):
            acc[b * TILE : (b + 1) * TILE] += sum(dot(a_side[b, u], side[b, u]) for u in range(3))

    acc[...] = dot(a_mid[1], pc[1])
    p_arrived("partner")
    acc[...] += dot(a_mid[u_in], pc[u_in])
    for dv in (-1, 1):
        p_arrived(("side", dv))
        p_start(("share", dv))
    p_arrived("outer")
    p_start(*relays)
    acc[...] += dot(a_mid[u_out], pc[u_out])
    p_arrived(*shares, *relays)
    add_sides(ps)

    for half in range(2):
        ax[half] = acc[:, half * 256 : (half + 1) * 256].astype(BF16)
    ax_copy = pltpu.make_async_remote_copy(
        src_ref=ax.at[1 - core],
        dst_ref=axp,
        send_sem=ax_sem.at[0],
        recv_sem=ax_sem.at[1],
        device_id=partner,
        device_id_type=MESH,
    )
    ax_copy.start()
    loads[2].wait()
    acc[...] = dot(ax[0], w_v[:256]) + dot(ax[1], w_v[256:])
    loads[3].wait()
    for r in range(0, 256, 32):
        p = acc[r : r + 32]
        sig = jax.nn.sigmoid(p)
        hid_v[r : r + 32] = (p * sig).astype(BF16)
        g = gh_v[r : r + 32].astype(F32)
        qc[1, r : r + 32] = (g * sig * (1.0 + p * (1.0 - sig))).astype(BF16)

    q_start("partner")

    own_part = dot_rows(ax[core], qc[1])
    part[...] = own_part.reshape(2, 8, 16, 512)
    ax_copy.wait()

    q_arrived("partner")
    part[...] += dot_rows(axp[...], qc[u_in]).reshape(2, 8, 16, 512)
    s1[...] = part[...].astype(BF16)

    first = ("y", "x")
    second = ("x", "y")
    at = {"x": x, "y": y, "z": z}

    def ar(stage, h, d, src, dst, dev):
        k = (stage * 2 + h) * 7 + d - 1
        return pltpu.make_async_remote_copy(
            src_ref=src,
            dst_ref=dst,
            send_sem=ar_ss.at[k],
            recv_sem=ar_rs.at[k],
            device_id=dev,
            device_id_type=MESH,
        )

    sent = []
    both = [(h, d) for d in (4, 3, 5, 2, 6, 1, 7) for h in range(2)]

    def run(stage, make):
        copies = []
        for h, d in both:
            c = make(stage, h, d)
            c.start()
            copies.append(c)
        sent.extend(copies)
        return copies

    def make1(stage, h, d):
        k, dev = peer(first[h], d)
        return ar(stage, h, d, s1.at[h, k], r1.at[h, d - 1], dev)

    copies = run(0, make1)
    q_start("outer", *sides)
    for c in copies:
        c.wait_recv()
    for h in range(2):
        total = part[h, at[first[h]]]
        for d in range(7):
            total = total + r1[h, d].astype(F32)
        for t in range(8):
            s2[h, t] = total[(t // 4) * 8 : (t // 4) * 8 + 8, (t % 4) * 128 : (t % 4) * 128 + 128]

    def make2(stage, h, d):
        k, dev = peer(second[h], d)
        return ar(stage, h, d, s2.at[h, k], r2.at[h, d - 1], dev)

    for c in run(1, make2):
        c.wait_recv()
    for h in range(2):
        total = s2[h, at[second[h]]]
        for d in range(7):
            total = total + r2[h, d]
        r3[h, z] = total

    def make3(stage, h, d):
        _, dev = peer("z", d)
        return ar(stage, h, d, r3.at[h, z], r3.at[h, z], dev)

    copies = run(2, make3)
    for dv in (-1, 1):
        q_arrived(("side", dv))
        q_start(("share", dv))
    q_arrived("outer")
    q_start(*relays)
    for c in copies:
        c.wait_recv()
    for h in range(2):
        total = r3[h, 0]
        for d in range(1, 8):
            total = total + r3[h, d]
        t2[h, at[second[h]]] = total

    def make4(stage, h, d):
        _, dev = peer(second[h], d)
        return ar(stage, h, d, t2.at[h, at[second[h]]], t2.at[h, at[second[h]]], dev)

    for c in run(3, make4):
        c.wait_recv()
    for h in range(2):
        lines = [jnp.concatenate([t2[h, 4 * r + k] for k in range(4)], axis=1) for r in range(2)]
        t1[h, at[first[h]]] = jnp.concatenate(lines, axis=0).astype(BF16)

    def make5(stage, h, d):
        _, dev = peer(first[h], d)
        return ar(stage, h, d, t1.at[h, at[first[h]]], t1.at[h, at[first[h]]], dev)

    copies = run(4, make5)

    def pair(h, d):
        k = lax.rem(at[first[h]] + (8 - d), 8)
        c = pltpu.make_async_remote_copy(
            src_ref=t1.at[h, k],
            dst_ref=tp.at[h, k],
            send_sem=tp_ss.at[h * 8 + d],
            recv_sem=tp_rs.at[h * 8 + d],
            device_id=partner,
            device_id_type=MESH,
        )
        c.start()
        return c

    pairs = [pair(h, 0) for h in range(2)]

    acc[...] = dot(a_mid[0], qc[0]) + dot(a_mid[1], qc[1]) + dot(a_mid[2], qc[2])
    q_arrived(*shares, *relays)
    add_sides(qs)
    back[...] = acc[...].astype(BF16)
    gf_v[...] = dot_cols(back[...], w_v[...]).astype(BF16)

    for (h, d), c in sorted(zip(both, copies), key=lambda e: (min(e[0][1], 8 - e[0][1]), e[0])):
        c.wait_recv()
        pairs.append(pair(h, d))
    gw_v[core] = t1[...].astype(F32) * scale
    for c in pairs:
        c.wait_recv()
    gw_v[1 - core] = tp[...].astype(F32) * scale

    for c in sent + pairs:
        c.wait_send()
    p_drained()
    q_drained()


def write_out(hid_v, gf_v, gw_v, hid_o, gf_o, gw_o, sem):
    copies = [
        pltpu.make_async_copy(gw_v, gw_o, sem.at[0]),
        pltpu.make_async_copy(hid_v, hid_o, sem.at[1]),
        pltpu.make_async_copy(gf_v, gf_o, sem.at[2]),
    ]
    for copy in copies:
        copy.start()
    for copy in copies:
        copy.wait()


def per_device(features, weight, edge_tiles, block_list, block_count, grad_hidden):
    rows, width = 2 * TILE, features.shape[3]
    nodes = LOOP * SECTION * rows
    local = pl.BlockSpec(memory_space=pltpu.VMEM)
    anywhere = pl.BlockSpec(memory_space=pl.ANY)
    scalars = pl.BlockSpec(memory_space=pltpu.SMEM)
    dma = pltpu.SemaphoreType.DMA
    vmem = pltpu.VMEM
    results = pl.pallas_call(
        functools.partial(kernel, 1.0 / math.sqrt(nodes)),
        out_shape=[
            pltpu.VMEM((rows, width), BF16),
            pltpu.VMEM((rows, width), BF16),
            pltpu.VMEM((2, 2, 8, 16, width), F32),
        ],
        in_specs=[scalars, scalars, anywhere, anywhere, anywhere, anywhere],
        out_specs=[local] * 3,
        scratch_shapes=[
            vmem((width, width), BF16),
            vmem((2, 9, TILE, TILE), BF16),
            vmem((rows, width), BF16),
            vmem((3, rows, rows), BF16),
            vmem((2, 3, TILE, TILE), BF16),
            vmem((rows, width), F32),
            vmem((3, rows, width), BF16),
            vmem((2, 3, TILE, width), BF16),
            vmem((3, rows, width), BF16),
            vmem((2, 3, TILE, width), BF16),
            vmem((2, rows, 256), BF16),
            vmem((rows, 256), BF16),
            vmem((rows, width), BF16),
            vmem((2, 8, 16, width), F32),
            vmem((2, 8, 16, width), BF16),
            vmem((2, 7, 16, width), BF16),
            vmem((2, 8, 8, 128), F32),
            vmem((2, 7, 8, 128), F32),
            vmem((2, 8, 8, 128), F32),
            vmem((2, 8, 8, 128), F32),
            vmem((2, 8, 16, width), BF16),
            vmem((2, 8, 16, width), BF16),
            dma((4,)),
            dma((8,)),
            dma((8,)),
            dma((8,)),
            dma((8,)),
            dma((2,)),
            dma((70,)),
            dma((70,)),
            dma((16,)),
            dma((16,)),
        ],
        compiler_params=pltpu.CompilerParams(collective_id=0, has_side_effects=True),
    )(
        block_list,
        block_count,
        features.reshape(rows, width),
        weight,
        edge_tiles.reshape(2, 9, TILE, TILE),
        grad_hidden.reshape(rows, width),
    )
    hidden, grad_features, grad_weight = pl.pallas_call(
        write_out,
        out_shape=[
            jax.ShapeDtypeStruct((rows, width), BF16),
            jax.ShapeDtypeStruct((rows, width), BF16),
            jax.ShapeDtypeStruct((2, 2, 8, 16, width), F32),
        ],
        in_specs=[local] * 3,
        out_specs=[anywhere] * 3,
        scratch_shapes=[dma((3,))],
    )(*[pltpu.with_memory_space_constraint(r, pltpu.VMEM) for r in results])
    grad_weight = grad_weight.reshape(width, width)
    return (hidden.reshape(features.shape), grad_features.reshape(features.shape), grad_weight)


def solution(mesh):
    placed = (
        P("loop", "section", None, None),
        P(),
        P("loop", "section", None, None, None),
        P("loop", "section", None),
        P("loop", "section"),
        P("loop", "section", None, None),
    )
    return jax.shard_map(
        per_device,
        mesh=mesh,
        in_specs=placed,
        out_specs=(P("loop", "section", None, None), P("loop", "section", None, None), P()),
        check_vma=False,
    )
```

time: 86.1 us -> 71.7 us (0.83)
  Pallas kernels: 81.3 us -> 70.9 us
  other arithmetic: 2.2 us -> 0 us
  local copies, waits for them, and re-layouts: 1.75 us -> 0 us
    pallas_call x1 -> x2, Pallas kernels: 81.3 us -> 70.9 us  [the longest x1 69.8 us: per_device(): pl.pallas_call(functools.partial(kernel, 1.0 / math.sqrt(nodes)), out_sha...]
    mul x1 -> x0, other arithmetic: 2.2 us -> none  [per_device(): total.reshape(width, width).astype(F32) * (1.0 / math.sqrt(nodes))]
    unnamed x6 -> x0, local copies, waits for them, and re-layouts: 1.75 us -> none
where the time goes in v2:
time: 71.7 us; the launch traced here: 71.6 us
  Pallas kernels  70.9 us (99%)
    pallas_call x1, Pallas kernels, per_device(): pl.pallas_call(functools.partial(kernel, 1.0 / math.sqrt(nodes)), out_sha...  69.8 us

profile of v2, /device:TPU:1, one launch (start us, length us, event | category | flops | bytes accessed | tf_op | source)
XLA Modules:
  0.0 71.6 jit_solution(15936515629441309533)
XLA Ops:
  0.6 69.8 %shard_map.85 = (bf16[256,512]{1,0:T(8,128)(2,1)S(1)}, bf16[256,512]{1,0:T(8,128)(2,1)S(1)}, f32[2,2,8,16,512]{4,3,2,1,0:T(8,128)S(1)}) custom-call(s32[1,2,9]{2,1,0:T(2,128)} %blist.1, s32[1,2]{1,0:T(1,128)} %bcount.1, bf16[256,512]{1,0:T(8,128)(2,1)} %bitcast.7, bf16[512,512]{1,0:T(8,128)(2,1)} %weight.1, bf16[2,9,128,128]{3,2,1,0:T(8,128)(2,1)} %bitcast.6, ...), custom_call_target="tpu_custom_call" | custom-call | tf_op jit(solution)/shard_map/pallas_call | solution.py:408
  70.4 1.2 %shard_map.86 = (bf16[256,512]{1,0:T(8,128)(2,1)}, bf16[256,512]{1,0:T(8,128)(2,1)}, f32[2,2,8,16,512]{4,3,2,1,0:T(8,128)}) custom-call(bf16[256,512]{1,0:T(8,128)(2,1)S(1)} %get-tuple-element.9.hid_v, bf16[256,512]{1,0:T(8,128)(2,1)S(1)} %get-tuple-element.10.gf_v, f32[2,2,8,16,512]{4,3,2,1,0:T(8,128)S(1)} %get-tuple-element.11.gw_v), custom_call_target="tpu_custom_call" | custom-call | tf_op jit(solution)/shard_map/pallas_call | solution.py:460

commit v3 on v2

--- a/solution.py
+++ b/solution.py
@@ -71,6 +71,7 @@
     ar_rs,
     tp_ss,
     tp_rs,
+    entered,
 ):
     L = lax.axis_index("loop")
     S = lax.axis_index("section")
@@ -111,10 +112,12 @@
         def _(dv=dv):
             pl.semaphore_signal(barrier, inc=1, device_id=(L, S + dv), device_id_type=MESH)
 
-    for axis in "xyz":
-        for d in range(1, 8):
-            _, dev = peer(axis, d)
-            pl.semaphore_signal(barrier, inc=1, device_id=dev, device_id_type=MESH)
+    def tell(sem, axes, hops):
+        for axis in axes:
+            for d in (hops, 8 - hops):
+                pl.semaphore_signal(sem, inc=1, device_id=peer(axis, d)[1], device_id_type=MESH)
+
+    tell(barrier, "xyz", 1)
 
     loads = [
         pltpu.make_async_copy(feat, pc.at[1], in_sem.at[0]),
@@ -154,10 +157,14 @@
         slot = {-1: 1, 1: 0}
         jobs = {
             "partner": (copy(0, mid.at[1], mid.at[u_out], partner), None, None),
-            "outer": (copy(1, mid.at[1], mid.at[u_in], (out_row, S)), has_out, has_out),
         }
         for i, dv in enumerate((-1, 1)):
             dev = (L, S + dv)
+            jobs["outer", dv] = (
+                copy((1, 8)[i], mid.at[1, cut[dv]], mid.at[u_in, cut[dv]], (out_row, S)),
+                has_out,
+                has_out,
+            )
             jobs["side", dv] = (
                 copy(2 + i, mid.at[1, cut[dv]], side.at[slot[dv], 1], dev),
                 has_side[dv],
@@ -195,11 +202,14 @@
     sides = (("side", -1), ("side", 1))
     relays = (("relay", -1), ("relay", 1))
     shares = (("share", -1), ("share", 1))
+    outers = (("outer", -1), ("outer", 1))
 
     loads[0].wait()
     greeted = has_out.astype(jnp.int32) + sum(has_side[dv].astype(jnp.int32) for dv in (-1, 1))
-    pl.semaphore_wait(barrier, 22 + greeted)
-    p_start("outer", *sides, "partner")
+    pl.semaphore_wait(barrier, 7 + greeted)
+    p_start(*outers, *sides, "partner")
+    tell(entered.at[0], "xy", 1)
+    tell(entered.at[1], "z", 1)
 
     loads[1].wait()
     for b in range(2):
@@ -225,8 +235,13 @@
     for dv in (-1, 1):
         p_arrived(("side", dv))
         p_start(("share", dv))
-    p_arrived("outer")
-    p_start(*relays)
+    for dv in (-1, 1):
+        p_arrived(("outer", dv))
+        p_start(("relay", dv))
+    pl.semaphore_wait(entered.at[0], 4)
+    tell(entered.at[2], "xy", 2)
+    pl.semaphore_wait(entered.at[1], 2)
+    tell(entered.at[3], "z", 2)
     acc[...] += dot(a_mid[u_out], pc[u_out])
     p_arrived(*shares, *relays)
     add_sides(ps)
@@ -293,8 +308,9 @@
         k, dev = peer(first[h], d)
         return ar(stage, h, d, s1.at[h, k], r1.at[h, d - 1], dev)
 
+    pl.semaphore_wait(entered.at[2], 4)
     copies = run(0, make1)
-    q_start("outer", *sides)
+    q_start(*outers, *sides)
     for c in copies:
         c.wait_recv()
     for h in range(2):
@@ -320,12 +336,11 @@
         _, dev = peer("z", d)
         return ar(stage, h, d, r3.at[h, z], r3.at[h, z], dev)
 
+    pl.semaphore_wait(entered.at[3], 2)
     copies = run(2, make3)
     for dv in (-1, 1):
         q_arrived(("side", dv))
         q_start(("share", dv))
-    q_arrived("outer")
-    q_start(*relays)
     for c in copies:
         c.wait_recv()
     for h in range(2):
@@ -338,7 +353,12 @@
         _, dev = peer(second[h], d)
         return ar(stage, h, d, t2.at[h, at[second[h]]], t2.at[h, at[second[h]]], dev)
 
-    for c in run(3, make4):
+    copies = run(3, make4)
+    for dv in (-1, 1):
+        q_arrived(("outer", dv))
+        q_start(("relay", dv))
+    acc[...] = dot(a_mid[0], qc[0]) + dot(a_mid[1], qc[1]) + dot(a_mid[2], qc[2])
+    for c in copies:
         c.wait_recv()
     for h in range(2):
         lines = [jnp.concatenate([t2[h, 4 * r + k] for k in range(4)], axis=1) for r in range(2)]
@@ -365,7 +385,6 @@
 
     pairs = [pair(h, 0) for h in range(2)]
 
-    acc[...] = dot(a_mid[0], qc[0]) + dot(a_mid[1], qc[1]) + dot(a_mid[2], qc[2])
     q_arrived(*shares, *relays)
     add_sides(qs)
     back[...] = acc[...].astype(BF16)
@@ -438,15 +457,16 @@
             vmem((2, 8, 16, width), BF16),
             vmem((2, 8, 16, width), BF16),
             dma((4,)),
-            dma((8,)),
-            dma((8,)),
-            dma((8,)),
-            dma((8,)),
+            dma((9,)),
+            dma((9,)),
+            dma((9,)),
+            dma((9,)),
             dma((2,)),
             dma((70,)),
             dma((70,)),
             dma((16,)),
             dma((16,)),
+            pltpu.SemaphoreType.REGULAR((4,)),
         ],
         compiler_params=pltpu.CompilerParams(collective_id=0, has_side_effects=True),
     )(

time: 71.7 us -> 72.1 us (level)
  no operation moved by 1% of the time
where the time goes in v3:
time: 72.1 us; the launch traced here: 71.9 us
  Pallas kernels  71.3 us (99%)
    pallas_call x1, Pallas kernels, per_device(): pl.pallas_call(functools.partial(kernel, 1.0 / math.sqrt(nodes)), out_sha...  70.1 us

profile of v3, /device:TPU:1, one launch (start us, length us, event | category | flops | bytes accessed | tf_op | source)
XLA Modules:
  0.0 71.9 jit_solution(13848450152488990701)
XLA Ops:
  0.6 70.1 %shard_map.85 = (bf16[256,512]{1,0:T(8,128)(2,1)S(1)}, bf16[256,512]{1,0:T(8,128)(2,1)S(1)}, f32[2,2,8,16,512]{4,3,2,1,0:T(8,128)S(1)}) custom-call(s32[1,2,9]{2,1,0:T(2,128)} %blist.1, s32[1,2]{1,0:T(1,128)} %bcount.1, bf16[256,512]{1,0:T(8,128)(2,1)} %bitcast.7, bf16[512,512]{1,0:T(8,128)(2,1)} %weight.1, bf16[2,9,128,128]{3,2,1,0:T(8,128)(2,1)} %bitcast.6, ...), custom_call_target="tpu_custom_call" | custom-call | tf_op jit(solution)/shard_map/pallas_call | solution.py:427
  70.8 1.2 %shard_map.86 = (bf16[256,512]{1,0:T(8,128)(2,1)}, bf16[256,512]{1,0:T(8,128)(2,1)}, f32[2,2,8,16,512]{4,3,2,1,0:T(8,128)}) custom-call(bf16[256,512]{1,0:T(8,128)(2,1)S(1)} %get-tuple-element.9.hid_v, bf16[256,512]{1,0:T(8,128)(2,1)S(1)} %get-tuple-element.10.gf_v, f32[2,2,8,16,512]{4,3,2,1,0:T(8,128)S(1)} %get-tuple-element.11.gw_v), custom_call_target="tpu_custom_call" | custom-call | tf_op jit(solution)/shard_map/pallas_call | solution.py:480

commit v4 on v3

--- a/solution.py
+++ b/solution.py
@@ -47,8 +47,10 @@
     acc,
     pc,
     ps,
+    pv,
     qc,
     qs,
+    qv,
     ax,
     axp,
     back,
@@ -80,8 +82,8 @@
     y = (L // (2 * NX)) * NYLO + S // NZ
     z = lax.rem(S, NZ)
 
-    def place(px, py, pz):
-        return ((py // NYLO) * (2 * NX) + px * 2 + core, lax.rem(py, NYLO) * NZ + pz)
+    def place(px, py, pz, pcore=core):
+        return ((py // NYLO) * (2 * NX) + px * 2 + pcore, lax.rem(py, NYLO) * NZ + pz)
 
     def peer(axis, d):
         if axis == "x":
@@ -102,9 +104,29 @@
     barrier = pltpu.get_barrier_semaphore()
     pl.semaphore_signal(barrier, inc=1, device_id=partner, device_id_type=MESH)
 
-    @pl.when(has_out)
+    rim = ((x == NX - 1) & (core == 1)) | ((x == 0) & (core == 0))
+    border, direct = has_out & rim, has_out & jnp.logical_not(rim)
+    way = lax.rem(y + 2 + 4 * core, NY) // (NY // 2)
+    step = 2 - 4 * way
+
+    def along(hops, across=False):
+        py = lax.rem(y + hops + NY, NY)
+        return place(NX - 1 - x, py, z, 1 - core) if across else place(x, py, z)
+
+    @pl.when(direct)
     def _():
         pl.semaphore_signal(barrier, inc=1, device_id=(out_row, S), device_id_type=MESH)
+
+    @pl.when(rim)
+    def _():
+        pl.semaphore_signal(barrier, inc=1, device_id=along(-step), device_id_type=MESH)
+        pl.semaphore_signal(barrier, inc=1, device_id=along(step, True), device_id_type=MESH)
+
+    @pl.when(border)
+    def _():
+        for hops in (-2, 2):
+            for across in (False, True):
+                pl.semaphore_signal(barrier, inc=1, device_id=along(hops, across), device_id_type=MESH)
 
     for dv in (-1, 1):
 
@@ -142,13 +164,13 @@
             def _(side=side, k=k):
                 side[k] = jnp.zeros((3, TILE, 512), BF16)
 
-    def halo(mid, side, ss, rs):
-        def copy(n, src, dst, dev):
+    def halo(mid, side, via, ss, rs):
+        def copy(n, src, dst, dev, m=None):
             return pltpu.make_async_remote_copy(
                 src_ref=src,
                 dst_ref=dst,
                 send_sem=ss.at[n],
-                recv_sem=rs.at[n],
+                recv_sem=rs.at[n if m is None else m],
                 device_id=dev,
                 device_id_type=MESH,
             )
@@ -158,13 +180,22 @@
         jobs = {
             "partner": (copy(0, mid.at[1], mid.at[u_out], partner), None, None),
         }
+        legs = []
+        onward = copy(
+            9,
+            via,
+            mid.at[u_in, pl.ds(pl.multiple_of(way * TILE, TILE), TILE)],
+            along(step, True),
+            1 + 7 * way,
+        )
         for i, dv in enumerate((-1, 1)):
             dev = (L, S + dv)
             jobs["outer", dv] = (
                 copy((1, 8)[i], mid.at[1, cut[dv]], mid.at[u_in, cut[dv]], (out_row, S)),
-                has_out,
+                direct,
                 has_out,
             )
+            legs.append(copy((1, 8)[i], mid.at[1, cut[dv]], via, along(-2 * dv), 9))
             jobs["side", dv] = (
                 copy(2 + i, mid.at[1, cut[dv]], side.at[slot[dv], 1], dev),
                 has_side[dv],
@@ -191,22 +222,43 @@
                 job, _, gets = jobs[key]
                 job.wait_recv() if gets is None else pl.when(gets)(job.wait_recv)
 
+        def start_border():
+            @pl.when(border)
+            def _():
+                for leg in legs:
+                    leg.start()
+
+        def pass_on():
+            @pl.when(rim)
+            def _():
+                legs[0].wait_recv()
+                onward.start()
+
         def drained():
             for job, sends, _ in jobs.values():
                 job.wait_send() if sends is None else pl.when(sends)(job.wait_send)
 
-        return start, arrived, drained
-
-    p_start, p_arrived, p_drained = halo(pc, ps, halo_ss, halo_rs)
-    q_start, q_arrived, q_drained = halo(qc, qs, ghalo_ss, ghalo_rs)
+            @pl.when(border)
+            def _():
+                for leg in legs:
+                    leg.wait_send()
+
+            pl.when(rim)(onward.wait_send)
+
+        return start, arrived, start_border, pass_on, drained
+
+    p_start, p_arrived, p_border, p_pass_on, p_drained = halo(pc, ps, pv, halo_ss, halo_rs)
+    q_start, q_arrived, q_border, q_pass_on, q_drained = halo(qc, qs, qv, ghalo_ss, ghalo_rs)
     sides = (("side", -1), ("side", 1))
     relays = (("relay", -1), ("relay", 1))
     shares = (("share", -1), ("share", 1))
     outers = (("outer", -1), ("outer", 1))
 
     loads[0].wait()
-    greeted = has_out.astype(jnp.int32) + sum(has_side[dv].astype(jnp.int32) for dv in (-1, 1))
+    greeted = direct.astype(jnp.int32) + 2 * rim.astype(jnp.int32) + 4 * border.astype(jnp.int32)
+    greeted = greeted + sum(has_side[dv].astype(jnp.int32) for dv in (-1, 1))
     pl.semaphore_wait(barrier, 7 + greeted)
+    p_border()
     p_start(*outers, *sides, "partner")
     tell(entered.at[0], "xy", 1)
     tell(entered.at[1], "z", 1)
@@ -232,6 +284,7 @@
     acc[...] = dot(a_mid[1], pc[1])
     p_arrived("partner")
     acc[...] += dot(a_mid[u_in], pc[u_in])
+    p_pass_on()
     for dv in (-1, 1):
         p_arrived(("side", dv))
         p_start(("share", dv))
@@ -310,6 +363,7 @@
 
     pl.semaphore_wait(entered.at[2], 4)
     copies = run(0, make1)
+    q_border()
     q_start(*outers, *sides)
     for c in copies:
         c.wait_recv()
@@ -324,7 +378,9 @@
         k, dev = peer(second[h], d)
         return ar(stage, h, d, s2.at[h, k], r2.at[h, d - 1], dev)
 
-    for c in run(1, make2):
+    copies = run(1, make2)
+    q_pass_on()
+    for c in copies:
         c.wait_recv()
     for h in range(2):
         total = s2[h, at[second[h]]]
@@ -442,8 +498,10 @@
             vmem((rows, width), F32),
             vmem((3, rows, width), BF16),
             vmem((2, 3, TILE, width), BF16),
+            vmem((TILE, width), BF16),
             vmem((3, rows, width), BF16),
             vmem((2, 3, TILE, width), BF16),
+            vmem((TILE, width), BF16),
             vmem((2, rows, 256), BF16),
             vmem((rows, 256), BF16),
             vmem((rows, width), BF16),
@@ -457,10 +515,10 @@
             vmem((2, 8, 16, width), BF16),
             vmem((2, 8, 16, width), BF16),
             dma((4,)),
-            dma((9,)),
-            dma((9,)),
-            dma((9,)),
-            dma((9,)),
+            dma((10,)),
+            dma((10,)),
+            dma((10,)),
+            dma((10,)),
             dma((2,)),
             dma((70,)),
             dma((70,)),

time: 72.1 us -> 71.9 us (level)
  no operation moved by 1% of the time
where the time goes in v4:
time: 71.9 us; the launch traced here: 71.7 us
  Pallas kernels  71.1 us (99%)
    pallas_call x1, Pallas kernels, per_device(): pl.pallas_call(functools.partial(kernel, 1.0 / math.sqrt(nodes)), out_sha...  69.9 us

profile of v4, /device:TPU:1, one launch (start us, length us, event | category | flops | bytes accessed | tf_op | source)
XLA Modules:
  0.0 71.7 jit_solution(14757037914609659025)
XLA Ops:
  0.6 69.9 %shard_map.85 = (bf16[256,512]{1,0:T(8,128)(2,1)S(1)}, bf16[256,512]{1,0:T(8,128)(2,1)S(1)}, f32[2,2,8,16,512]{4,3,2,1,0:T(8,128)S(1)}) custom-call(s32[1,2,9]{2,1,0:T(2,128)} %blist.1, s32[1,2]{1,0:T(1,128)} %bcount.1, bf16[256,512]{1,0:T(8,128)(2,1)} %bitcast.7, bf16[512,512]{1,0:T(8,128)(2,1)} %weight.1, bf16[2,9,128,128]{3,2,1,0:T(8,128)(2,1)} %bitcast.6, ...), custom_call_target="tpu_custom_call" | custom-call | tf_op jit(solution)/shard_map/pallas_call | solution.py:483
  70.6 1.2 %shard_map.86 = (bf16[256,512]{1,0:T(8,128)(2,1)}, bf16[256,512]{1,0:T(8,128)(2,1)}, f32[2,2,8,16,512]{4,3,2,1,0:T(8,128)}) custom-call(bf16[256,512]{1,0:T(8,128)(2,1)S(1)} %get-tuple-element.9.hid_v, bf16[256,512]{1,0:T(8,128)(2,1)S(1)} %get-tuple-element.10.gf_v, f32[2,2,8,16,512]{4,3,2,1,0:T(8,128)S(1)} %get-tuple-element.11.gw_v), custom_call_target="tpu_custom_call" | custom-call | tf_op jit(solution)/shard_map/pallas_call | solution.py:538

commit v5 on v4

--- a/solution.py
+++ b/solution.py
@@ -30,8 +30,8 @@
 
 def kernel(
     scale,
-    blist,
-    bcount,
+    blist_h,
+    bcount_h,
     feat,
     weight,
     edge,
@@ -57,12 +57,11 @@
     part,
     s1,
     r1,
-    s2,
-    r2,
-    r3,
-    t2,
+    rx,
     t1,
     tp,
+    blist,
+    bcount,
     in_sem,
     halo_ss,
     halo_rs,
@@ -146,6 +145,8 @@
         pltpu.make_async_copy(edge, e_v, in_sem.at[1]),
         pltpu.make_async_copy(weight, w_v, in_sem.at[2]),
         pltpu.make_async_copy(gh, gh_v, in_sem.at[3]),
+        pltpu.make_async_copy(blist_h, blist, in_sem.at[4]),
+        pltpu.make_async_copy(bcount_h, bcount, in_sem.at[5]),
     ]
     for load in loads:
         load.start()
@@ -263,7 +264,8 @@
     tell(entered.at[0], "xy", 1)
     tell(entered.at[1], "z", 1)
 
-    loads[1].wait()
+    for k in (1, 4, 5):
+        loads[k].wait()
     for b in range(2):
         bits = jnp.int32(0)
         for k in range(9):
@@ -285,12 +287,17 @@
     p_arrived("partner")
     acc[...] += dot(a_mid[u_in], pc[u_in])
     p_pass_on()
+
+    def corners():
+        for dv in (-1, 1):
+            p_arrived(("outer", dv))
+            p_start(("relay", dv))
+
+    pl.when(direct)(corners)
     for dv in (-1, 1):
         p_arrived(("side", dv))
         p_start(("share", dv))
-    for dv in (-1, 1):
-        p_arrived(("outer", dv))
-        p_start(("relay", dv))
+    pl.when(border)(corners)
     pl.semaphore_wait(entered.at[0], 4)
     tell(entered.at[2], "xy", 2)
     pl.semaphore_wait(entered.at[1], 2)
@@ -334,8 +341,7 @@
     second = ("x", "y")
     at = {"x": x, "y": y, "z": z}
 
-    def ar(stage, h, d, src, dst, dev):
-        k = (stage * 2 + h) * 7 + d - 1
+    def ar(k, src, dst, dev):
         return pltpu.make_async_remote_copy(
             src_ref=src,
             dst_ref=dst,
@@ -346,23 +352,44 @@
         )
 
     sent = []
-    both = [(h, d) for d in (4, 3, 5, 2, 6, 1, 7) for h in range(2)]
-
-    def run(stage, make):
-        copies = []
-        for h, d in both:
-            c = make(stage, h, d)
+    far_first = (4, 3, 5, 2, 6, 1, 7)
+    both = [(h, d) for d in far_first for h in range(2)]
+    quarters = [(h, c) for h in range(2) for c in range(2)]
+
+    def run(copies):
+        for c in copies:
             c.start()
-            copies.append(c)
         sent.extend(copies)
         return copies
 
-    def make1(stage, h, d):
+    def scatter(h, d):
         k, dev = peer(first[h], d)
-        return ar(stage, h, d, s1.at[h, k], r1.at[h, d - 1], dev)
+        return ar(h * 7 + d - 1, s1.at[h, k], r1.at[h, d - 1], dev)
+
+    def axis_of(stage, h, c):
+        return "z" if stage == c else second[h]
+
+    def exchange(stage, h, c, d):
+        _, dev = peer(axis_of(stage, h, c), d)
+        slot = rx.at[stage, h, c, at[axis_of(stage, h, c)]]
+        return ar(14 + ((stage * 2 + h) * 2 + c) * 7 + d - 1, slot, slot, dev)
+
+    def exchange_all(stage):
+        return run([exchange(stage, h, c, d) for d in far_first for h, c in quarters])
+
+    def summed(stage, h, c):
+        total = rx[stage, h, c, 0].astype(F32)
+        for k in range(1, 8):
+            total = total + rx[stage, h, c, k].astype(F32)
+        return total.astype(BF16)
+
+    def gather(h, d):
+        _, dev = peer(first[h], d)
+        slot = t1.at[h, at[first[h]]]
+        return ar(70 + h * 7 + d - 1, slot, slot, dev)
 
     pl.semaphore_wait(entered.at[2], 4)
-    copies = run(0, make1)
+    copies = run([scatter(h, d) for h, d in both])
     q_border()
     q_start(*outers, *sides)
     for c in copies:
@@ -371,60 +398,32 @@
         total = part[h, at[first[h]]]
         for d in range(7):
             total = total + r1[h, d].astype(F32)
-        for t in range(8):
-            s2[h, t] = total[(t // 4) * 8 : (t // 4) * 8 + 8, (t % 4) * 128 : (t % 4) * 128 + 128]
-
-    def make2(stage, h, d):
-        k, dev = peer(second[h], d)
-        return ar(stage, h, d, s2.at[h, k], r2.at[h, d - 1], dev)
-
-    copies = run(1, make2)
+        for c in range(2):
+            rx[1, h, c, at[axis_of(1, h, c)]] = total[:, c * 256 : (c + 1) * 256].astype(BF16)
+
+    pl.semaphore_wait(entered.at[3], 2)
+    copies = exchange_all(1)
     q_pass_on()
-    for c in copies:
-        c.wait_recv()
-    for h in range(2):
-        total = s2[h, at[second[h]]]
-        for d in range(7):
-            total = total + r2[h, d]
-        r3[h, z] = total
-
-    def make3(stage, h, d):
-        _, dev = peer("z", d)
-        return ar(stage, h, d, r3.at[h, z], r3.at[h, z], dev)
-
-    pl.semaphore_wait(entered.at[3], 2)
-    copies = run(2, make3)
     for dv in (-1, 1):
         q_arrived(("side", dv))
         q_start(("share", dv))
     for c in copies:
         c.wait_recv()
-    for h in range(2):
-        total = r3[h, 0]
-        for d in range(1, 8):
-            total = total + r3[h, d]
-        t2[h, at[second[h]]] = total
-
-    def make4(stage, h, d):
-        _, dev = peer(second[h], d)
-        return ar(stage, h, d, t2.at[h, at[second[h]]], t2.at[h, at[second[h]]], dev)
-
-    copies = run(3, make4)
-    for dv in (-1, 1):
-        q_arrived(("outer", dv))
-        q_start(("relay", dv))
-    acc[...] = dot(a_mid[0], qc[0]) + dot(a_mid[1], qc[1]) + dot(a_mid[2], qc[2])
+    for h, c in quarters:
+        rx[0, h, c, at[axis_of(0, h, c)]] = summed(1, h, c)
+    copies = exchange_all(0)
+
+    def q_corners():
+        for dv in (-1, 1):
+            q_arrived(("outer", dv))
+            q_start(("relay", dv))
+
+    pl.when(direct)(q_corners)
     for c in copies:
         c.wait_recv()
-    for h in range(2):
-        lines = [jnp.concatenate([t2[h, 4 * r + k] for k in range(4)], axis=1) for r in range(2)]
-        t1[h, at[first[h]]] = jnp.concatenate(lines, axis=0).astype(BF16)
-
-    def make5(stage, h, d):
-        _, dev = peer(first[h], d)
-        return ar(stage, h, d, t1.at[h, at[first[h]]], t1.at[h, at[first[h]]], dev)
-
-    copies = run(4, make5)
+    for h, c in quarters:
+        t1[h, at[first[h]], :, c * 256 : (c + 1) * 256] = summed(0, h, c)
+    copies = run([gather(h, d) for h, d in both])
 
     def pair(h, d):
         k = lax.rem(at[first[h]] + (8 - d), 8)
@@ -440,15 +439,17 @@
         return c
 
     pairs = [pair(h, 0) for h in range(2)]
-
+    pl.when(border)(q_corners)
+    acc[...] = dot(a_mid[0], qc[0]) + dot(a_mid[1], qc[1]) + dot(a_mid[2], qc[2])
+
+    for (h, d), c in sorted(zip(both, copies), key=lambda e: (min(e[0][1], 8 - e[0][1]), e[0])):
+        c.wait_recv()
+        pairs.append(pair(h, d))
     q_arrived(*shares, *relays)
     add_sides(qs)
     back[...] = acc[...].astype(BF16)
     gf_v[...] = dot_cols(back[...], w_v[...]).astype(BF16)
 
-    for (h, d), c in sorted(zip(both, copies), key=lambda e: (min(e[0][1], 8 - e[0][1]), e[0])):
-        c.wait_recv()
-        pairs.append(pair(h, d))
     gw_v[core] = t1[...].astype(F32) * scale
     for c in pairs:
         c.wait_recv()
@@ -477,7 +478,6 @@
     nodes = LOOP * SECTION * rows
     local = pl.BlockSpec(memory_space=pltpu.VMEM)
     anywhere = pl.BlockSpec(memory_space=pl.ANY)
-    scalars = pl.BlockSpec(memory_space=pltpu.SMEM)
     dma = pltpu.SemaphoreType.DMA
     vmem = pltpu.VMEM
     results = pl.pallas_call(
@@ -487,7 +487,7 @@
             pltpu.VMEM((rows, width), BF16),
             pltpu.VMEM((2, 2, 8, 16, width), F32),
         ],
-        in_specs=[scalars, scalars, anywhere, anywhere, anywhere, anywhere],
+        in_specs=[anywhere] * 6,
         out_specs=[local] * 3,
         scratch_shapes=[
             vmem((width, width), BF16),
@@ -508,20 +508,19 @@
             vmem((2, 8, 16, width), F32),
             vmem((2, 8, 16, width), BF16),
             vmem((2, 7, 16, width), BF16),
-            vmem((2, 8, 8, 128), F32),
-            vmem((2, 7, 8, 128), F32),
-            vmem((2, 8, 8, 128), F32),
-            vmem((2, 8, 8, 128), F32),
+            vmem((2, 2, 2, 8, 16, 256), BF16),
             vmem((2, 8, 16, width), BF16),
             vmem((2, 8, 16, width), BF16),
-            dma((4,)),
+            pltpu.SMEM((1, 2, 9), jnp.int32),
+            pltpu.SMEM((1, 2), jnp.int32),
+            dma((6,)),
             dma((10,)),
             dma((10,)),
             dma((10,)),
             dma((10,)),
             dma((2,)),
-            dma((70,)),
-            dma((70,)),
+            dma((84,)),
+            dma((84,)),
             dma((16,)),
             dma((16,)),
             pltpu.SemaphoreType.REGULAR((4,)),

time: 71.9 us -> 69.9 us (0.972)
  Pallas kernels: 71.1 us -> 69.1 us
    pallas_call x1, Pallas kernels: 69.9 us -> 67.9 us  [per_device(): pl.pallas_call(functools.partial(kernel, 1.0 / math.sqrt(nodes)), out_sha...]
where the time goes in v5:
time: 69.9 us; the launch traced here: 69.7 us
  Pallas kernels  69.1 us (99%)
    pallas_call x1, Pallas kernels, per_device(): pl.pallas_call(functools.partial(kernel, 1.0 / math.sqrt(nodes)), out_sha...  67.9 us

profile of v5, /device:TPU:1, one launch (start us, length us, event | category | flops | bytes accessed | tf_op | source)
XLA Modules:
  0.0 69.7 jit_solution(16852255879100183921)
XLA Ops:
  0.6 67.9 %shard_map.85 = (bf16[256,512]{1,0:T(8,128)(2,1)S(1)}, bf16[256,512]{1,0:T(8,128)(2,1)S(1)}, f32[2,2,8,16,512]{4,3,2,1,0:T(8,128)S(1)}) custom-call(s32[1,2,9]{2,1,0:T(2,128)} %blist_h.1, s32[1,2]{1,0:T(1,128)} %bcount_h.1, bf16[256,512]{1,0:T(8,128)(2,1)} %bitcast.7, bf16[512,512]{1,0:T(8,128)(2,1)} %weight.1, bf16[2,9,128,128]{3,2,1,0:T(8,128)(2,1)} %bitcast.6, ...), custom_call_target="tpu_custom_call" | custom-call | tf_op jit(solution)/shard_map/pallas_call | solution.py:483
  68.6 1.2 %shard_map.86 = (bf16[256,512]{1,0:T(8,128)(2,1)}, bf16[256,512]{1,0:T(8,128)(2,1)}, f32[2,2,8,16,512]{4,3,2,1,0:T(8,128)}) custom-call(bf16[256,512]{1,0:T(8,128)(2,1)S(1)} %get-tuple-element.9.hid_v, bf16[256,512]{1,0:T(8,128)(2,1)S(1)} %get-tuple-element.10.gf_v, f32[2,2,8,16,512]{4,3,2,1,0:T(8,128)S(1)} %get-tuple-element.11.gw_v), custom_call_target="tpu_custom_call" | custom-call | tf_op jit(solution)/shard_map/pallas_call | solution.py:537

commit v6 on v5

--- a/solution.py
+++ b/solution.py
@@ -47,10 +47,8 @@
     acc,
     pc,
     ps,
-    pv,
     qc,
     qs,
-    qv,
     ax,
     axp,
     back,
@@ -81,8 +79,8 @@
     y = (L // (2 * NX)) * NYLO + S // NZ
     z = lax.rem(S, NZ)
 
-    def place(px, py, pz, pcore=core):
-        return ((py // NYLO) * (2 * NX) + px * 2 + pcore, lax.rem(py, NYLO) * NZ + pz)
+    def place(px, py, pz):
+        return ((py // NYLO) * (2 * NX) + px * 2 + core, lax.rem(py, NYLO) * NZ + pz)
 
     def peer(axis, d):
         if axis == "x":
@@ -103,29 +101,9 @@
     barrier = pltpu.get_barrier_semaphore()
     pl.semaphore_signal(barrier, inc=1, device_id=partner, device_id_type=MESH)
 
-    rim = ((x == NX - 1) & (core == 1)) | ((x == 0) & (core == 0))
-    border, direct = has_out & rim, has_out & jnp.logical_not(rim)
-    way = lax.rem(y + 2 + 4 * core, NY) // (NY // 2)
-    step = 2 - 4 * way
-
-    def along(hops, across=False):
-        py = lax.rem(y + hops + NY, NY)
-        return place(NX - 1 - x, py, z, 1 - core) if across else place(x, py, z)
-
-    @pl.when(direct)
+    @pl.when(has_out)
     def _():
         pl.semaphore_signal(barrier, inc=1, device_id=(out_row, S), device_id_type=MESH)
-
-    @pl.when(rim)
-    def _():
-        pl.semaphore_signal(barrier, inc=1, device_id=along(-step), device_id_type=MESH)
-        pl.semaphore_signal(barrier, inc=1, device_id=along(step, True), device_id_type=MESH)
-
-    @pl.when(border)
-    def _():
-        for hops in (-2, 2):
-            for across in (False, True):
-                pl.semaphore_signal(barrier, inc=1, device_id=along(hops, across), device_id_type=MESH)
 
     for dv in (-1, 1):
 
@@ -165,13 +143,13 @@
             def _(side=side, k=k):
                 side[k] = jnp.zeros((3, TILE, 512), BF16)
 
-    def halo(mid, side, via, ss, rs):
-        def copy(n, src, dst, dev, m=None):
+    def halo(mid, side, ss, rs):
+        def copy(n, src, dst, dev):
             return pltpu.make_async_remote_copy(
                 src_ref=src,
                 dst_ref=dst,
                 send_sem=ss.at[n],
-                recv_sem=rs.at[n if m is None else m],
+                recv_sem=rs.at[n],
                 device_id=dev,
                 device_id_type=MESH,
             )
@@ -181,22 +159,13 @@
         jobs = {
             "partner": (copy(0, mid.at[1], mid.at[u_out], partner), None, None),
         }
-        legs = []
-        onward = copy(
-            9,
-            via,
-            mid.at[u_in, pl.ds(pl.multiple_of(way * TILE, TILE), TILE)],
-            along(step, True),
-            1 + 7 * way,
-        )
         for i, dv in enumerate((-1, 1)):
             dev = (L, S + dv)
             jobs["outer", dv] = (
                 copy((1, 8)[i], mid.at[1, cut[dv]], mid.at[u_in, cut[dv]], (out_row, S)),
-                direct,
+                has_out,
                 has_out,
             )
-            legs.append(copy((1, 8)[i], mid.at[1, cut[dv]], via, along(-2 * dv), 9))
             jobs["side", dv] = (
                 copy(2 + i, mid.at[1, cut[dv]], side.at[slot[dv], 1], dev),
                 has_side[dv],
@@ -223,43 +192,22 @@
                 job, _, gets = jobs[key]
                 job.wait_recv() if gets is None else pl.when(gets)(job.wait_recv)
 
-        def start_border():
-            @pl.when(border)
-            def _():
-                for leg in legs:
-                    leg.start()
-
-        def pass_on():
-            @pl.when(rim)
-            def _():
-                legs[0].wait_recv()
-                onward.start()
-
         def drained():
             for job, sends, _ in jobs.values():
                 job.wait_send() if sends is None else pl.when(sends)(job.wait_send)
 
-            @pl.when(border)
-            def _():
-                for leg in legs:
-                    leg.wait_send()
-
-            pl.when(rim)(onward.wait_send)
-
-        return start, arrived, start_border, pass_on, drained
-
-    p_start, p_arrived, p_border, p_pass_on, p_drained = halo(pc, ps, pv, halo_ss, halo_rs)
-    q_start, q_arrived, q_border, q_pass_on, q_drained = halo(qc, qs, qv, ghalo_ss, ghalo_rs)
+        return start, arrived, drained
+
+    p_start, p_arrived, p_drained = halo(pc, ps, halo_ss, halo_rs)
+    q_start, q_arrived, q_drained = halo(qc, qs, ghalo_ss, ghalo_rs)
     sides = (("side", -1), ("side", 1))
     relays = (("relay", -1), ("relay", 1))
     shares = (("share", -1), ("share", 1))
     outers = (("outer", -1), ("outer", 1))
 
     loads[0].wait()
-    greeted = direct.astype(jnp.int32) + 2 * rim.astype(jnp.int32) + 4 * border.astype(jnp.int32)
-    greeted = greeted + sum(has_side[dv].astype(jnp.int32) for dv in (-1, 1))
+    greeted = has_out.astype(jnp.int32) + sum(has_side[dv].astype(jnp.int32) for dv in (-1, 1))
     pl.semaphore_wait(barrier, 7 + greeted)
-    p_border()
     p_start(*outers, *sides, "partner")
     tell(entered.at[0], "xy", 1)
     tell(entered.at[1], "z", 1)
@@ -279,32 +227,29 @@
             else:
                 a_side[b, u] = tile
 
-    def add_sides(side):
+    def add_side(side, u):
         for b in range(2):
-            acc[b * TILE : (b + 1) * TILE] += sum(dot(a_side[b, u], side[b, u]) for u in range(3))
+            acc[b * TILE : (b + 1) * TILE] += dot(a_side[b, u], side[b, u])
 
     acc[...] = dot(a_mid[1], pc[1])
     p_arrived("partner")
     acc[...] += dot(a_mid[u_in], pc[u_in])
-    p_pass_on()
-
-    def corners():
-        for dv in (-1, 1):
-            p_arrived(("outer", dv))
-            p_start(("relay", dv))
-
-    pl.when(direct)(corners)
-    for dv in (-1, 1):
-        p_arrived(("side", dv))
-        p_start(("share", dv))
-    pl.when(border)(corners)
     pl.semaphore_wait(entered.at[0], 4)
     tell(entered.at[2], "xy", 2)
     pl.semaphore_wait(entered.at[1], 2)
     tell(entered.at[3], "z", 2)
+    for dv in (-1, 1):
+        p_arrived(("outer", dv))
+        p_start(("relay", dv))
+    for dv in (-1, 1):
+        p_arrived(("side", dv))
+        p_start(("share", dv))
+    add_side(ps, 1)
     acc[...] += dot(a_mid[u_out], pc[u_out])
-    p_arrived(*shares, *relays)
-    add_sides(ps)
+    p_arrived(*shares)
+    add_side(ps, u_in)
+    p_arrived(*relays)
+    add_side(ps, u_out)
 
     for half in range(2):
         ax[half] = acc[:, half * 256 : (half + 1) * 256].astype(BF16)
@@ -390,7 +335,6 @@
 
     pl.semaphore_wait(entered.at[2], 4)
     copies = run([scatter(h, d) for h, d in both])
-    q_border()
     q_start(*outers, *sides)
     for c in copies:
         c.wait_recv()
@@ -403,7 +347,6 @@
 
     pl.semaphore_wait(entered.at[3], 2)
     copies = exchange_all(1)
-    q_pass_on()
     for dv in (-1, 1):
         q_arrived(("side", dv))
         q_start(("share", dv))
@@ -412,13 +355,9 @@
     for h, c in quarters:
         rx[0, h, c, at[axis_of(0, h, c)]] = summed(1, h, c)
     copies = exchange_all(0)
-
-    def q_corners():
-        for dv in (-1, 1):
-            q_arrived(("outer", dv))
-            q_start(("relay", dv))
-
-    pl.when(direct)(q_corners)
+    for dv in (-1, 1):
+        q_arrived(("outer", dv))
+        q_start(("relay", dv))
     for c in copies:
         c.wait_recv()
     for h, c in quarters:
@@ -439,14 +378,16 @@
         return c
 
     pairs = [pair(h, 0) for h in range(2)]
-    pl.when(border)(q_corners)
     acc[...] = dot(a_mid[0], qc[0]) + dot(a_mid[1], qc[1]) + dot(a_mid[2], qc[2])
+    q_arrived(*shares)
+    add_side(qs, 1)
+    add_side(qs, u_in)
 
     for (h, d), c in sorted(zip(both, copies), key=lambda e: (min(e[0][1], 8 - e[0][1]), e[0])):
         c.wait_recv()
         pairs.append(pair(h, d))
-    q_arrived(*shares, *relays)
-    add_sides(qs)
+    q_arrived(*relays)
+    add_side(qs, u_out)
     back[...] = acc[...].astype(BF16)
     gf_v[...] = dot_cols(back[...], w_v[...]).astype(BF16)
 
@@ -498,10 +439,8 @@
             vmem((rows, width), F32),
             vmem((3, rows, width), BF16),
             vmem((2, 3, TILE, width), BF16),
-            vmem((TILE, width), BF16),
             vmem((3, rows, width), BF16),
             vmem((2, 3, TILE, width), BF16),
-            vmem((TILE, width), BF16),
             vmem((2, rows, 256), BF16),
             vmem((rows, 256), BF16),
             vmem((rows, width), BF16),
@@ -514,10 +453,10 @@
             pltpu.SMEM((1, 2, 9), jnp.int32),
             pltpu.SMEM((1, 2), jnp.int32),
             dma((6,)),
-            dma((10,)),
-            dma((10,)),
-            dma((10,)),
-            dma((10,)),
+            dma((9,)),
+            dma((9,)),
+            dma((9,)),
+            dma((9,)),
             dma((2,)),
             dma((84,)),
             dma((84,)),

time: 69.9 us -> 67.1 us (0.960)
  Pallas kernels: 69.1 us -> 66.3 us
    pallas_call x1, Pallas kernels: 67.9 us -> 65.2 us  [per_device(): pl.pallas_call(functools.partial(kernel, 1.0 / math.sqrt(nodes)), out_sha...]
where the time goes in v6:
time: 67.1 us; the launch traced here: 67 us
  Pallas kernels  66.3 us (99%)
    pallas_call x1, Pallas kernels, per_device(): pl.pallas_call(functools.partial(kernel, 1.0 / math.sqrt(nodes)), out_sha...  65.2 us

profile of v6, /device:TPU:1, one launch (start us, length us, event | category | flops | bytes accessed | tf_op | source)
XLA Modules:
  0.0 67.0 jit_solution(802449450211986839)
XLA Ops:
  0.6 65.2 %shard_map.85 = (bf16[256,512]{1,0:T(8,128)(2,1)S(1)}, bf16[256,512]{1,0:T(8,128)(2,1)S(1)}, f32[2,2,8,16,512]{4,3,2,1,0:T(8,128)S(1)}) custom-call(s32[1,2,9]{2,1,0:T(2,128)} %blist_h.1, s32[1,2]{1,0:T(1,128)} %bcount_h.1, bf16[256,512]{1,0:T(8,128)(2,1)} %bitcast.7, bf16[512,512]{1,0:T(8,128)(2,1)} %weight.1, bf16[2,9,128,128]{3,2,1,0:T(8,128)(2,1)} %bitcast.6, ...), custom_call_target="tpu_custom_call" | custom-call | tf_op jit(solution)/shard_map/pallas_call | solution.py:424
  65.8 1.2 %shard_map.86 = (bf16[256,512]{1,0:T(8,128)(2,1)}, bf16[256,512]{1,0:T(8,128)(2,1)}, f32[2,2,8,16,512]{4,3,2,1,0:T(8,128)}) custom-call(bf16[256,512]{1,0:T(8,128)(2,1)S(1)} %get-tuple-element.9.hid_v, bf16[256,512]{1,0:T(8,128)(2,1)S(1)} %get-tuple-element.10.gf_v, f32[2,2,8,16,512]{4,3,2,1,0:T(8,128)S(1)} %get-tuple-element.11.gw_v), custom_call_target="tpu_custom_call" | custom-call | tf_op jit(solution)/shard_map/pallas_call | solution.py:476

commit v7 on v6

--- a/solution.py
+++ b/solution.py
@@ -355,9 +355,14 @@
     for h, c in quarters:
         rx[0, h, c, at[axis_of(0, h, c)]] = summed(1, h, c)
     copies = exchange_all(0)
-    for dv in (-1, 1):
-        q_arrived(("outer", dv))
-        q_start(("relay", dv))
+
+    def q_corners():
+        for dv in (-1, 1):
+            q_arrived(("outer", dv))
+            q_start(("relay", dv))
+
+    border = ((x == NX - 1) & (core == 1)) | ((x == 0) & (core == 0))
+    pl.when(jnp.logical_not(border))(q_corners)
     for c in copies:
         c.wait_recv()
     for h, c in quarters:
@@ -378,6 +383,7 @@
         return c
 
     pairs = [pair(h, 0) for h in range(2)]
+    pl.when(border)(q_corners)
     acc[...] = dot(a_mid[0], qc[0]) + dot(a_mid[1], qc[1]) + dot(a_mid[2], qc[2])
     q_arrived(*shares)
     add_side(qs, 1)

time: 67.1 us -> 66.5 us (level)
    pallas_call x1, Pallas kernels: 65.2 us -> 64.5 us  [per_device(): pl.pallas_call(functools.partial(kernel, 1.0 / math.sqrt(nodes)), out_sha...]
where the time goes in v7:
time: 66.5 us; the launch traced here: 66.3 us
  Pallas kernels  65.7 us (99%)
    pallas_call x1, Pallas kernels, per_device(): pl.pallas_call(functools.partial(kernel, 1.0 / math.sqrt(nodes)), out_sha...  64.5 us

profile of v7, /device:TPU:1, one launch (start us, length us, event | category | flops | bytes accessed | tf_op | source)
XLA Modules:
  0.0 66.3 jit_solution(10091289338805684249)
XLA Ops:
  0.6 64.5 %shard_map.85 = (bf16[256,512]{1,0:T(8,128)(2,1)S(1)}, bf16[256,512]{1,0:T(8,128)(2,1)S(1)}, f32[2,2,8,16,512]{4,3,2,1,0:T(8,128)S(1)}) custom-call(s32[1,2,9]{2,1,0:T(2,128)} %blist_h.1, s32[1,2]{1,0:T(1,128)} %bcount_h.1, bf16[256,512]{1,0:T(8,128)(2,1)} %bitcast.7, bf16[512,512]{1,0:T(8,128)(2,1)} %weight.1, bf16[2,9,128,128]{3,2,1,0:T(8,128)(2,1)} %bitcast.6, ...), custom_call_target="tpu_custom_call" | custom-call | tf_op jit(solution)/shard_map/pallas_call | solution.py:430
  65.1 1.2 %shard_map.86 = (bf16[256,512]{1,0:T(8,128)(2,1)}, bf16[256,512]{1,0:T(8,128)(2,1)}, f32[2,2,8,16,512]{4,3,2,1,0:T(8,128)}) custom-call(bf16[256,512]{1,0:T(8,128)(2,1)S(1)} %get-tuple-element.9.hid_v, bf16[256,512]{1,0:T(8,128)(2,1)S(1)} %get-tuple-element.10.gf_v, f32[2,2,8,16,512]{4,3,2,1,0:T(8,128)S(1)} %get-tuple-element.11.gw_v), custom_call_target="tpu_custom_call" | custom-call | tf_op jit(solution)/shard_map/pallas_call | solution.py:482
